TPU v7x, 512 devices: a whole 4x8x8 slice. The times are simulated.
512 devices in a mesh: lat: 16 (over z, x_hi), lon: 32 (over y, x_lo, core).
Axes of the slice: x: 4 (x_hi: 2, x_lo: 2; x = x_hi * 2 + x_lo), y: 8, z: 8, core: 2. Of those that a mesh axis runs over, the one named last changes fastest.
Arguments:
- frame: bfloat16 [256, 512, 256], P('lat', 'lon'), may hold values from -64 to 64
- weight_qkv: bfloat16 [256, 768], replicated, may hold values from -0.375 to 0.375
- weight_proj: bfloat16 [256, 256], replicated, may hold values from -0.375 to 0.375
- gain_attn: float32 [256], replicated, may hold values from 0.5 to 1.5
- weight_up: bfloat16 [256, 1024], replicated, may hold values from -0.375 to 0.375
- weight_down: bfloat16 [1024, 256], replicated, may hold values from -0.1875 to 0.1875
- gain_mlp: float32 [256], replicated, may hold values from 0.5 to 1.5
- cotangent: bfloat16 [256, 512, 256], P('lat', 'lon'), may hold values from -6 to 6
Outputs:
- block_out: bfloat16 [256, 512, 256], P('lat', 'lon')
- grad_frame: bfloat16 [256, 512, 256], P('lat', 'lon')
- grad_qkv: bfloat16 [256, 768], replicated
- grad_proj: bfloat16 [256, 256], replicated
- grad_up: bfloat16 [256, 1024], replicated
- grad_down: bfloat16 [1024, 256], replicated
- grad_gain_attn: float32 [256], replicated
- grad_gain_mlp: float32 [256], replicated
All inputs are finite; a program needn't handle non-finite values.
Results may differ from a plain program's by a relative error of at most 0.012.
The roundings to bfloat16 on the way count: a program that leaves them out, or rounds other values in their place, can miss the bound.
Values may be sent and summed in bfloat16 or wider, within the bound.
No kernel may reach another device: no remote copies, remote signals or barrier semaphores. Data moves between devices by JAX's collectives and lax.ppermute only.
A program may use at most 128 MiB of HBM per device.

v0:
```python
import jax
import jax.numpy as jnp
from jax import lax
from jax.sharding import PartitionSpec as P

HEADS = 8
RADIUS = 6


epsilon = 1e-06
cubic_term = 0.044715
gelu_root = 0.7978845608028654
negative_big = -1e30


def padded_2(x, sides, width, wrap):
    for axis, dim in sides:
        devices, length = (lax.axis_size(axis), x.shape[dim])
        up = [(i, (i + 1) % devices) for i in range(devices if wrap else devices - 1)]
        down = [(j, i) for i, j in up]
        last = lax.slice_in_dim(x, length - width, length, axis=dim)
        first = lax.slice_in_dim(x, 0, width, axis=dim)
        before = lax.ppermute(last, axis, up)
        after = lax.ppermute(first, axis, down)
        x = jnp.concatenate([before, x, after], axis=dim)
    return x


def gelu_pair(upward):
    tangent = jnp.tanh(gelu_root * (upward + cubic_term * upward * upward * upward))
    activated = 0.5 * upward * (1.0 + tangent)
    derivative = 0.5 * (1.0 + tangent) + 0.5 * upward * (1.0 - tangent * tangent) * gelu_root * (
        1.0 + 3.0 * cubic_term * upward * upward
    )
    return (activated, derivative)


def rms_factor(field):
    return lax.rsqrt(jnp.mean(field * field, axis=-1, keepdims=True) + epsilon)


def norm_backward(incoming, field, factor):
    mean_term = jnp.mean(incoming * field, axis=-1, keepdims=True)
    return factor * (incoming - field * factor * factor * mean_term)


def contract_rows(left, right):
    return lax.dot_general(
        left, right, (((0,), (0,)), ((), ())), preferred_element_type=jnp.float32
    )


def contract_cols(left, right):
    return lax.dot_general(
        left, right, (((1,), (1,)), ((), ())), preferred_element_type=jnp.float32
    )


def row_strips(padded, rows, span):
    return jnp.stack(
        [lax.slice_in_dim(padded, offset, offset + rows, axis=0) for offset in range(span)], axis=1
    )


def unstrip(strip_sum, rows, span):
    total = jnp.zeros((rows + span - 1,) + strip_sum.shape[2:], strip_sum.dtype)
    for offset in range(span):
        total = total.at[offset : offset + rows].add(strip_sum[:, offset])
    return total


def fold_rims(field, axis, length, radius):
    middle = lax.slice_in_dim(field, 2 * radius, 2 * radius + length, axis=axis)
    front = lax.slice_in_dim(field, 0, radius, axis=axis)
    back = lax.slice_in_dim(field, length + 3 * radius, length + 4 * radius, axis=axis)
    widths_front = [(0, 0)] * field.ndim
    widths_front[axis] = (0, length - radius)
    widths_back = [(0, 0)] * field.ndim
    widths_back[axis] = (length - radius, 0)
    return middle + jnp.pad(front, widths_front) + jnp.pad(back, widths_back)


def band_strips(padded, rows, span, heads):
    strips = row_strips(padded, rows, span)
    return strips.reshape(rows, span * padded.shape[1], heads, padded.shape[2] // heads)


def on_device(
    frame, weight_qkv, weight_proj, gain_attn, weight_up, weight_down, gain_mlp, cotangent
):
    lat_rows, lon_cols, width = frame.shape
    heads = HEADS
    head_size = width // heads
    radius = RADIUS
    span = 2 * radius + 1
    head_scale = head_size ** (-0.5)
    pad_rows = lat_rows + 2 * radius
    pad_cols = lon_cols + 2 * radius
    band = span * pad_cols
    local_tokens = lat_rows * lon_cols
    lat_total = lat_rows * lax.axis_size("lat")
    tokens_all = lat_total * lon_cols * lax.axis_size("lon")
    grad_scale = tokens_all ** (-0.5)
    lat_first = lax.axis_index("lat") * lat_rows
    row_global = lat_first + jnp.arange(lat_rows)[:, None] + jnp.arange(span)[None, :] - radius
    row_ok = (row_global >= 0) & (row_global < lat_total)
    col_gap = jnp.arange(pad_cols)[None, :] - radius - jnp.arange(lon_cols)[:, None]
    near = jnp.abs(col_gap) <= radius
    valid = (row_ok[:, None, :, None] & near[None, :, None, :]).reshape(lat_rows, 1, lon_cols, band)
    flat = frame.reshape(local_tokens, width)
    projected = jnp.dot(flat, weight_qkv, preferred_element_type=jnp.float32).astype(jnp.bfloat16)
    queries = projected[:, :width]
    pairs = projected[:, width:].reshape(lat_rows, lon_cols, 2 * width)
    widened = padded_2(pairs, (("lon", 1),), radius, True)
    margined = padded_2(widened, (("lat", 0),), radius, False)
    pair_pad = margined.reshape(-1, 2 * width)
    queries4 = queries.reshape(lat_rows, lon_cols, heads, head_size)
    keys_pad = pair_pad[:, :width].reshape(pad_rows, pad_cols, width)
    values_pad = pair_pad[:, width:].reshape(pad_rows, pad_cols, width)
    key_strip = band_strips(keys_pad, lat_rows, span, heads)
    value_strip = band_strips(values_pad, lat_rows, span, heads)
    scores = (
        jnp.einsum("ichd,inhd->ihcn", queries4, key_strip, preferred_element_type=jnp.float32)
        * head_scale
    )
    scores = jnp.where(valid, scores, negative_big)
    peak = jnp.max(scores, axis=3, keepdims=True)
    expo = jnp.exp(scores - peak)
    total = jnp.sum(expo, axis=3, keepdims=True)
    probs = expo / total
    probs_bf = probs.astype(jnp.bfloat16)
    attended = (
        jnp.einsum("ihcn,inhd->ichd", probs_bf, value_strip, preferred_element_type=jnp.float32)
        .astype(jnp.bfloat16)
        .reshape(local_tokens, width)
    )
    proj = jnp.dot(attended, weight_proj, preferred_element_type=jnp.float32)
    factor_one = rms_factor(proj)
    mid = (flat.astype(jnp.float32) + proj * factor_one * gain_attn).astype(jnp.bfloat16)
    upward = jnp.dot(mid, weight_up, preferred_element_type=jnp.float32)
    activated, derivative = gelu_pair(upward)
    hidden = activated.astype(jnp.bfloat16)
    downward = jnp.dot(hidden, weight_down, preferred_element_type=jnp.float32)
    factor_two = rms_factor(downward)
    block_out = (mid.astype(jnp.float32) + downward * factor_two * gain_mlp).astype(jnp.bfloat16)
    incoming = cotangent.reshape(local_tokens, width).astype(jnp.float32)
    local_gain_mlp = jnp.sum(incoming * downward * factor_two, axis=0)
    d_down = norm_backward(incoming * gain_mlp, downward, factor_two).astype(jnp.bfloat16)
    local_down = contract_rows(hidden, d_down)
    d_up = (contract_cols(d_down, weight_down) * derivative).astype(jnp.bfloat16)
    local_up = contract_rows(mid, d_up)
    d_mid = incoming + contract_cols(d_up, weight_up)
    local_gain_attn = jnp.sum(d_mid * proj * factor_one, axis=0)
    d_proj = norm_backward(d_mid * gain_attn, proj, factor_one).astype(jnp.bfloat16)
    local_proj = contract_rows(attended, d_proj)
    d_attended = contract_cols(d_proj, weight_proj).astype(jnp.bfloat16)
    d_attended4 = d_attended.reshape(lat_rows, lon_cols, heads, head_size)
    d_probs = jnp.einsum(
        "ichd,inhd->ihcn", d_attended4, value_strip, preferred_element_type=jnp.float32
    )
    d_weighted = jnp.sum(probs * d_probs, axis=3, keepdims=True)
    d_scores = (probs * (d_probs - d_weighted) * head_scale).astype(jnp.bfloat16)
    d_queries = jnp.einsum(
        "ihcn,inhd->ichd", d_scores, key_strip, preferred_element_type=jnp.float32
    ).reshape(local_tokens, width)
    key_terms = jnp.einsum(
        "ihcn,ichd->inhd", d_scores, queries4, preferred_element_type=jnp.float32
    ).reshape(lat_rows, span, pad_cols, width)
    value_terms = jnp.einsum(
        "ihcn,ichd->inhd", probs_bf, d_attended4, preferred_element_type=jnp.float32
    ).reshape(lat_rows, span, pad_cols, width)
    pair_grads = unstrip(jnp.concatenate([key_terms, value_terms], axis=3), lat_rows, span)
    widened_grads = padded_2(pair_grads.astype(jnp.bfloat16), (("lon", 1),), radius, True).astype(
        pair_grads.dtype
    )
    margined_grads = padded_2(
        widened_grads.astype(jnp.bfloat16), (("lat", 0),), radius, False
    ).astype(widened_grads.dtype)
    owned = fold_rims(fold_rims(margined_grads, 0, lat_rows, radius), 1, lon_cols, radius).reshape(
        local_tokens, 2 * width
    )
    d_projected = jnp.concatenate([d_queries, owned], axis=1).astype(jnp.bfloat16)
    local_qkv = contract_rows(flat, d_projected)
    grad_frame = (d_mid + contract_cols(d_projected, weight_qkv)).astype(jnp.bfloat16)
    sum_qkv, sum_proj, sum_up, sum_down, sum_gain_attn, sum_gain_mlp = lax.psum(
        (local_qkv, local_proj, local_up, local_down, local_gain_attn, local_gain_mlp),
        ("lat", "lon"),
    )
    return (
        block_out.reshape(lat_rows, lon_cols, width),
        grad_frame.reshape(lat_rows, lon_cols, width),
        (sum_qkv * grad_scale).astype(jnp.bfloat16),
        (sum_proj * grad_scale).astype(jnp.bfloat16),
        (sum_up * grad_scale).astype(jnp.bfloat16),
        (sum_down * grad_scale).astype(jnp.bfloat16),
        sum_gain_attn * grad_scale,
        sum_gain_mlp * grad_scale,
    )


def solution(mesh):
    return jax.shard_map(
        on_device,
        mesh=mesh,
        in_specs=(P("lat", "lon", None), P(), P(), P(), P(), P(), P(), P("lat", "lon", None)),
        out_specs=(P("lat", "lon", None), P("lat", "lon", None), P(), P(), P(), P(), P(), P()),
        check_vma=False,
    )
```

profile of v0, /device:TPU:1, one launch (start us, length us, event | category | flops | bytes accessed | tf_op | source)
XLA Modules:
  0.0 695.3 jit_solution(14059497985502001922)
XLA Ops:
  8.7 4.5 collective-permute-start
  13.2 6.2 collective-permute-start.1
  20.5 3.6 collective-permute-start.2
  26.7 5.3 collective-permute-done.3
  79.0 18.8 %copy.50 = bf16[16,13,28,256]{2,1,3,0:T(8,128)(2,1)} copy(bf16[16,13,28,256]{3,2,0,1:T(8,128)(2,1)} %constant_dynamic-update-slice_fusion.13) | data formatting | bytes 5963776 | tf_op jit(solution)/shard_map/reshape | solution.py:85
  97.9 21.2 %reshape.626 = bf16[16,364,8,32]{1,3,2,0:T(8,128)(2,1)} reshape(bf16[16,13,28,256]{2,1,3,0:T(8,128)(2,1)} %copy.50) | data formatting | bytes 5963776 | tf_op jit(solution)/shard_map/reshape | solution.py:85
  127.8 18.8 %copy.49 = bf16[16,13,28,256]{2,1,3,0:T(8,128)(2,1)} copy(bf16[16,13,28,256]{3,2,0,1:T(8,128)(2,1)} %constant_dynamic-update-slice_fusion) | data formatting | bytes 5963776 | tf_op jit(solution)/shard_map/reshape | solution.py:85
  146.6 21.2 %reshape.625 = bf16[16,364,8,32]{1,3,2,0:T(8,128)(2,1)} reshape(bf16[16,13,28,256]{2,1,3,0:T(8,128)(2,1)} %copy.49) | data formatting | bytes 5963776 | tf_op jit(solution)/shard_map/reshape | solution.py:85
  170.5 3.8 fusion.78
  181.2 4.3 fusion.49
  185.5 17.5 %fusion.20 = bf16[16,16,8,32]{3,1,2,0:T(8,128)(2,1)} fusion(bf16[16,364,8,32]{1,3,2,0:T(8,128)(2,1)} %reshape.626, f32[16,8,16,364]{3,2,1,0:T(8,128)} %fusion.49, f32[16,8,16,364]{3,2,1,0:T(8,128)} %copy-done.5, f32[16,8,16]{2,1,0:T(8,128)S(1)} %get-tuple-element.226), kind=kOutput, calls=%fused_computation.27 | convolution fusion | flops 52996460 | bytes 9084928 | tf_op jit(solution)/shard_map/ihcn,inhd->ichd/dot_general | solution.py:163
  203.0 17.6 %convolution_bitcast_fusion.1 = f32[16,364,8,32]{1,3,2,0:T(8,128)} fusion(f32[16,8,16,364]{3,2,1,0:T(8,128)} %fusion.49, bf16[16,16,8,32]{3,2,1,0:T(8,128)(2,1)S(1)} %reshape.602, f32[16,8,16,364]{3,2,1,0:T(8,128)} %copy-done.5, f32[16,8,16]{2,1,0:T(8,128)S(1)} %get-tuple-element.226), kind=kOutput, calls=%fused_computation.8 | convolution fusion | flops 52930924 | bytes 12066816 | tf_op jit(solution)/shard_map/ihcn,ichd->inhd/dot_general | solution.py:166
  220.6 5.6 convolution_bitcast_fusion
  226.2 20.3 %copy.46 = f32[16,364,8,32]{3,2,0,1:T(8,128)} copy(f32[16,364,8,32]{1,3,2,0:T(8,128)} %convolution_bitcast_fusion) | data formatting | bytes 11927552 | tf_op jit(solution)/shard_map/ihcn,ichd->inhd/transpose | solution.py:169
  246.5 16.9 %reshape.609 = f32[16,13,28,256]{3,0,2,1:T(8,128)} reshape(f32[16,364,8,32]{3,2,0,1:T(8,128)} %copy.46) | data formatting | bytes 11927552 | tf_op jit(solution)/shard_map/reshape | solution.py:171
  263.4 20.3 %copy.44 = f32[16,364,8,32]{3,2,0,1:T(8,128)} copy(f32[16,364,8,32]{1,3,2,0:T(8,128)} %convolution_bitcast_fusion.1) | data formatting | bytes 11927552 | tf_op jit(solution)/shard_map/ihcn,ichd->inhd/transpose | solution.py:166
  283.8 16.8 %reshape.608 = f32[16,13,28,256]{3,0,2,1:T(8,128)} reshape(f32[16,364,8,32]{3,2,0,1:T(8,128)} %copy.44) | data formatting | bytes 11927552 | tf_op jit(solution)/shard_map/reshape | solution.py:168
  300.6 3.8 constant_dynamic-update-slice_fusion.27
  307.0 4.1 copy-done.2
  355.7 5.2 collective-permute-start.5
  363.7 8.5 %collective-permute-start.6 = (bf16[6,40,512]{2,0,1:T(8,128)(2,1)}, bf16[6,40,512]{2,0,1:T(8,128)(2,1)S(1)}, u32[]{:S(2)}, u32[]{:S(2)}) collective-permute-start(bf16[6,40,512]{2,0,1:T(8,128)(2,1)} %get-tuple-element.190), channel_id=1, source_target_pairs={{0,32},{32,64},{64,96},{96,128},{128,160},{160,192},{192,224},{224... | collective-permute-start | bytes 737288 | tf_op jit(solution)/shard_map/ppermute | solution.py:23
  376.5 9.6 %collective-permute-done.6 = bf16[6,40,512]{2,0,1:T(8,128)(2,1)S(1)} collective-permute-done((bf16[6,40,512]{2,0,1:T(8,128)(2,1)}, bf16[6,40,512]{2,0,1:T(8,128)(2,1)S(1)}, u32[]{:S(2)}, u32[]{:S(2)}) %collective-permute-start.6) | collective-permute-done | bytes 245792 | tf_op jit(solution)/shard_map/ppermute | solution.py:23
  389.1 106.7 %all-reduce.3 = (f32[256]{0:T(256)S(1)}, f32[256]{0:T(256)S(1)}) all-reduce(f32[256]{0:T(256)S(1)} %get-tuple-element.180, f32[256]{0:T(256)S(1)} %get-tuple-element.182), channel_id=1, replica_groups=mesh['lat'=16,'lon'=32] {'lat','lon'}, use_global_device_ids=true, to_apply=%region_12.13 | all-reduce | flops 512 | bytes 4096 | tf_op jit(solution)/shard_map/psum | solution.py:185
  497.3 184.1 %all-reduce.7.cloned.1.call-done = (f32[256,768]{0,1:T(8,128)}, f32[256,256]{1,0:T(8,128)}, f32[256,1024]{1,0:T(8,128)}, f32[1024,256]{1,0:T(8,128)}) async-done(((f32[256,768]{0,1:T(8,128)}, f32[256,256]{1,0:T(8,128)}, f32[256,1024]{1,0:T(8,128)}, f32[1024,256]{1,0:T(8,128)}), (f32[256,768]{0,1:T(8,128)}, f32[256,256]{1,0:T(8,128)}, f32[256,1024]{1,0:T(8,128)}, ...) | async-done | bytes 3145744 | tf_op jit(solution)/shard_map/psum | solution.py:185
  (234 shorter events, 135.4 us)
Async XLA Ops:
  7.2 169.7 %copy-start = (bf16[256,1024]{1,0:T(8,128)(2,1)S(1)}, bf16[256,1024]{1,0:T(8,128)(2,1)}, u32[]{:S(2)}) copy-start(bf16[256,1024]{1,0:T(8,128)(2,1)} %param.38) | copy-start | bytes 1572868
  7.2 674.1 %all-reduce.7.cloned.1.call-start = ((), (), s32[]{:S(2)}) async-start(), calls=%async_computation | async-start | bytes 6291456 | tf_op jit(solution)/shard_map/psum | solution.py:185
  8.7 11.4 %collective-permute-start = (bf16[16,6,512]{2,1,0:T(8,128)(2,1)S(1)}, bf16[16,6,512]{2,1,0:T(8,128)(2,1)S(1)}, u32[]{:S(2)}, u32[]{:S(2)}) collective-permute-start(bf16[16,6,512]{2,1,0:T(8,128)(2,1)S(1)} %get-tuple-element.224), channel_id=1, source_target_pairs={{0,1},{1,2},{2,3},{3,4},{4,5},{5,6},{6,7},{7,8},{8,9},{9,10},{10,1... | collective-permute-start | bytes 294920 | tf_op jit(solution)/shard_map/ppermute | solution.py:23
  13.2 7.1 %collective-permute-start.1 = (bf16[16,6,512]{2,1,0:T(8,128)(2,1)S(1)}, bf16[16,6,512]{2,1,0:T(8,128)(2,1)S(1)}, u32[]{:S(2)}, u32[]{:S(2)}) collective-permute-start(bf16[16,6,512]{2,1,0:T(8,128)(2,1)S(1)} %get-tuple-element.225), channel_id=1, source_target_pairs={{1,0},{2,1},{3,2},{4,3},{5,4},{6,5},{7,6},{8,7},{9,8},{10,9},{11,1... | collective-permute-start | bytes 294920 | tf_op jit(solution)/shard_map/ppermute | solution.py:24
  20.5 6.2 collective-permute-start.2
  24.1 7.9 %collective-permute-start.3 = (bf16[6,28,512]{2,1,0:T(8,128)(2,1)S(1)}, bf16[6,28,512]{2,1,0:T(8,128)(2,1)S(1)}, u32[]{:S(2)}, u32[]{:S(2)}) collective-permute-start(bf16[6,28,512]{2,1,0:T(8,128)(2,1)S(1)} %get-tuple-element.221), channel_id=1, source_target_pairs={{32,0},{64,32},{96,64},{128,96},{160,128},{192,160},{224,192},{256... | collective-permute-start | bytes 516104 | tf_op jit(solution)/shard_map/ppermute | solution.py:24
  37.4 19.4 %copy-start.31 = (bf16[448,256]{1,0:T(8,128)(2,1)S(1)}, bf16[448,256]{1,0:T(8,128)(2,1)}, u32[]{:S(2)}) copy-start(bf16[448,256]{1,0:T(8,128)(2,1)} %get-tuple-element.206) | copy-start | bytes 688132
  37.4 20.1 %copy-start.30 = (bf16[448,256]{1,0:T(8,128)(2,1)S(1)}, bf16[448,256]{1,0:T(8,128)(2,1)}, u32[]{:S(2)}) copy-start(bf16[448,256]{1,0:T(8,128)(2,1)} %get-tuple-element.207) | copy-start | bytes 688132
  38.1 19.4 %copy-start.29 = (bf16[448,256]{1,0:T(8,128)(2,1)S(1)}, bf16[448,256]{1,0:T(8,128)(2,1)}, u32[]{:S(2)}) copy-start(bf16[448,256]{1,0:T(8,128)(2,1)} %get-tuple-element.208) | copy-start | bytes 688132
  63.7 12.4 %copy-start.23 = (bf16[16,1,28,256]{3,2,0,1:T(8,128)(2,1)S(1)}, bf16[16,1,28,256]{3,2,0,1:T(8,128)(2,1)}, u32[]{:S(2)}) copy-start(bf16[16,1,28,256]{3,2,0,1:T(8,128)(2,1)} %stack.107) | copy-start | bytes 688132
  63.7 13.1 %copy-start.21 = (bf16[16,1,28,256]{3,2,0,1:T(8,128)(2,1)S(1)}, bf16[16,1,28,256]{3,2,0,1:T(8,128)(2,1)}, u32[]{:S(2)}) copy-start(bf16[16,1,28,256]{3,2,0,1:T(8,128)(2,1)} %stack.108) | copy-start | bytes 688132
  63.7 13.9 %copy-start.19 = (bf16[16,1,28,256]{3,2,0,1:T(8,128)(2,1)S(1)}, bf16[16,1,28,256]{3,2,0,1:T(8,128)(2,1)}, u32[]{:S(2)}) copy-start(bf16[16,1,28,256]{3,2,0,1:T(8,128)(2,1)} %stack.109) | copy-start | bytes 688132
  63.7 14.6 %copy-start.17 = (bf16[16,1,28,256]{3,2,0,1:T(8,128)(2,1)S(1)}, bf16[16,1,28,256]{3,2,0,1:T(8,128)(2,1)}, u32[]{:S(2)}) copy-start(bf16[16,1,28,256]{3,2,0,1:T(8,128)(2,1)} %stack.110) | copy-start | bytes 688132
  352.5 21.3 %copy-start.7 = (bf16[256,1024]{1,0:T(8,128)(2,1)S(1)}, bf16[256,1024]{1,0:T(8,128)(2,1)}, u32[]{:S(2)}) copy-start(bf16[256,1024]{1,0:T(8,128)(2,1)} %copy-done.6) | copy-start | bytes 1572868
  352.5 9.9 %collective-permute-start.4 = (bf16[28,6,512]{2,0,1:T(8,128)(2,1)S(1)}, bf16[28,6,512]{2,0,1:T(8,128)(2,1)S(1)}, u32[]{:S(2)}, u32[]{:S(2)}) collective-permute-start(bf16[28,6,512]{2,0,1:T(8,128)(2,1)S(1)} %get-tuple-element.192), channel_id=1, source_target_pairs={{0,1},{1,2},{2,3},{3,4},{4,5},{5,6},{6,7},{7,8},{8,9},{9,10},{10,1... | collective-permute-start | bytes 516104 | tf_op jit(solution)/shard_map/ppermute | solution.py:23
  355.7 19.4 %copy-start.33 = (bf16[16,16,8,32]{3,1,2,0:T(8,128)(2,1)S(1)}, bf16[16,16,8,32]{3,1,2,0:T(8,128)(2,1)}, u32[]{:S(2)}) copy-start(bf16[16,16,8,32]{3,1,2,0:T(8,128)(2,1)} %fusion.20) | copy-start | bytes 393220
  355.7 7.1 %collective-permute-start.5 = (bf16[28,6,512]{2,0,1:T(8,128)(2,1)S(1)}, bf16[28,6,512]{2,0,1:T(8,128)(2,1)S(1)}, u32[]{:S(2)}, u32[]{:S(2)}) collective-permute-start(bf16[28,6,512]{2,0,1:T(8,128)(2,1)S(1)} %get-tuple-element.193), channel_id=1, source_target_pairs={{1,0},{2,1},{3,2},{4,3},{5,4},{6,5},{7,6},{8,7},{9,8},{10,9},{11,1... | collective-permute-start | bytes 516104 | tf_op jit(solution)/shard_map/ppermute | solution.py:24
  362.4 13.1 %copy-start.10 = (bf16[256,256]{1,0:T(8,128)(2,1)S(1)}, bf16[256,256]{1,0:T(8,128)(2,1)}, u32[]{:S(2)}) copy-start(bf16[256,256]{1,0:T(8,128)(2,1)} %copy-done.9) | copy-start | bytes 393220
  362.4 13.1 %copy-start.12 = (bf16[256,256]{1,0:T(8,128)(2,1)S(1)}, bf16[256,256]{1,0:T(8,128)(2,1)}, u32[]{:S(2)}) copy-start(bf16[256,256]{1,0:T(8,128)(2,1)} %copy-done.11) | copy-start | bytes 393220
  363.7 22.4 %collective-permute-start.6 = (bf16[6,40,512]{2,0,1:T(8,128)(2,1)}, bf16[6,40,512]{2,0,1:T(8,128)(2,1)S(1)}, u32[]{:S(2)}, u32[]{:S(2)}) collective-permute-start(bf16[6,40,512]{2,0,1:T(8,128)(2,1)} %get-tuple-element.190), channel_id=1, source_target_pairs={{0,32},{32,64},{64,96},{96,128},{128,160},{160,192},{192,224},{224... | collective-permute-start | bytes 737288 | tf_op jit(solution)/shard_map/ppermute | solution.py:23
  372.2 13.9 %collective-permute-start.7 = (bf16[6,40,512]{2,0,1:T(8,128)(2,1)}, bf16[6,40,512]{2,0,1:T(8,128)(2,1)S(1)}, u32[]{:S(2)}, u32[]{:S(2)}) collective-permute-start(bf16[6,40,512]{2,0,1:T(8,128)(2,1)} %get-tuple-element.191), channel_id=1, source_target_pairs={{32,0},{64,32},{96,64},{128,96},{160,128},{192,160},{224,192},{256... | collective-permute-start | bytes 737288 | tf_op jit(solution)/shard_map/ppermute | solution.py:24
  387.5 108.8 %copy-start.16 = (f32[256,256]{1,0:T(8,128)S(1)}, f32[256,256]{1,0:T(8,128)}, u32[]{:S(2)}) copy-start(f32[256,256]{1,0:T(8,128)} %copy-done.15) | copy-start | bytes 786436
  387.5 108.8 %copy-start.35 = (bf16[256,768]{1,0:T(8,128)(2,1)S(1)}, bf16[256,768]{1,0:T(8,128)(2,1)}, u32[]{:S(2)}) copy-start(bf16[256,768]{1,0:T(8,128)(2,1)} %param.35) | copy-start | bytes 1179652
  495.7 192.5 %copy-start.1 = (bf16[256,1024]{1,0:T(8,128)(2,1)S(1)}, bf16[256,1024]{1,0:T(8,128)(2,1)}, u32[]{:S(2)}) copy-start(bf16[256,1024]{1,0:T(8,128)(2,1)} %param.38) | copy-start | bytes 1572868
  (28 other events, 112.3 us)
Sparse Core Ops, SparseCore 0:
  389.2 292.1 all-reduce.6
where the time goes:
time: 707 us; the launch traced here: 695 us
  local copies, waits for them, and re-layouts  249 us (35%)
  waiting for transfers between devices  200 us (28%)
  blocking collectives  107 us (15%)
  matrix products  58.8 us (8%)
  starting transfers between devices  33.9 us (5%)
  other arithmetic  31.2 us (4%)
  between operations  15.2 us (2%)
    psum x1, waiting for transfers between devices, on_device(): lax.psum((local_qkv, local_proj, local_up, local_down, local_gain_attn, l...  184 us
    psum x1, blocking collectives, on_device(): lax.psum((local_qkv, local_proj, local_up, local_down, local_gain_attn, l...  107 us
    reshape x4, local copies, waits for them, and re-layouts, band_strips(): strips.reshape(rows, span * padded.shape[1], heads, padded.shape[2] // he...  80.1 us
    unnamed x112, local copies, waits for them, and re-layouts  33.7 us
    another operation x28, local copies, waits for them, and re-layouts, row_strips(): jnp.stack([lax.slice_in_dim(padded, offset, offset + rows, axis=0) for of...  29 us
    scatter-add x12, local copies, waits for them, and re-layouts, unstrip(): total = total.at[offset:offset + rows].add(strip_sum[:, offset])  25.4 us
    transpose x1, local copies, waits for them, and re-layouts, on_device(): jnp.einsum('ihcn,ichd->inhd', probs_bf, d_attended4, preferred_element_ty...  20.3 us
    transpose x1, local copies, waits for them, and re-layouts, on_device(): jnp.einsum('ihcn,ichd->inhd', d_scores, queries4, preferred_element_type=...  20.3 us
  transfers between devices with their start and end apart: 9, of which 6 were waited for; matrix products, arithmetic and copies ran while one was open for 1% of the time, Pallas kernels for 0%

commit v1 on v0

v1 whole, which is shorter than its diff:
```python
import functools

import jax
import jax.numpy as jnp
from jax import lax
from jax.experimental import pallas as pl
from jax.experimental.pallas import tpu as pltpu
from jax.sharding import PartitionSpec as P

HEADS = 8
RADIUS = 6
EDGE = 8

epsilon = 1e-06
cubic_term = 0.044715
gelu_root = 0.7978845608028654
negative_big = -1e30

F32 = jnp.float32
BF16 = jnp.bfloat16


def nn(left, right):
    return lax.dot_general(left, right, (((1,), (0,)), ((), ())), preferred_element_type=F32)


def nt(left, right):
    return lax.dot_general(left, right, (((1,), (1,)), ((), ())), preferred_element_type=F32)


def gelu_pair(upward):
    tangent = jnp.tanh(gelu_root * (upward + cubic_term * upward * upward * upward))
    activated = 0.5 * upward * (1.0 + tangent)
    derivative = 0.5 * (1.0 + tangent) + 0.5 * upward * (1.0 - tangent * tangent) * gelu_root * (
        1.0 + 3.0 * cubic_term * upward * upward
    )
    return (activated, derivative)


def rms_factor(field):
    return lax.rsqrt(jnp.mean(field * field, axis=-1, keepdims=True) + epsilon)


def norm_backward(incoming, field, factor):
    mean_term = jnp.mean(incoming * field, axis=-1, keepdims=True)
    return factor * (incoming - field * factor * factor * mean_term)


def local_kernel(
    dims,
    where_ref,
    frame_ref,
    wide_ref,
    top_ref,
    bottom_ref,
    wqkv_ref,
    wproj_ref,
    gain_attn_ref,
    wup_ref,
    wdown_ref,
    gain_mlp_ref,
    cot_ref,
    block_out_ref,
    d_mid_ref,
    dq_ref,
    up_ref,
    down_ref,
    centre_ref,
    grads_ref,
    gains_ref,
    halo,
    keys,
    values,
    keys_t,
    values_t,
    stack_q,
    stack_o,
    bias,
    probs,
    probs_bf,
    d_scores,
    att_t,
    dq_t,
    hidden,
    slope,
    pair_grads,
):
    rows, cols, lat_total = dims["rows"], dims["cols"], dims["lat_total"]
    heads, size, width, ff = HEADS, dims["width"] // HEADS, dims["width"], dims["ff"]
    across = cols + 2 * EDGE
    block_rows = 128 // cols
    blocks = rows // block_rows
    reach = (block_rows + 2 * RADIUS) * across
    step = block_rows * across
    pairs = heads // 2
    head_scale = size ** (-0.5)
    lat_first = where_ref[0]
    core = where_ref[1]
    side = (core, 1 - core)

    def put(index, value):
        half, row = divmod(index, 6)
        grads_ref[side[half], row * 512 : row * 512 + 256, :] = value[:, :128]
        grads_ref[side[half], row * 512 + 256 : row * 512 + 512, :] = value[:, 128:]

    rim = RADIUS * across
    inner = rows * across
    halo[0:rim, :] = top_ref[...]
    halo[rim : rim + inner, :] = wide_ref[...]
    halo[rim + inner : inner + 2 * rim, :] = bottom_ref[...]
    grid = halo[...]
    key32 = nn(grid, wqkv_ref[:, width : 2 * width])
    keys[...] = key32.astype(BF16)
    keys_t[...] = key32.T.astype(BF16)
    value32 = nn(grid, wqkv_ref[:, 2 * width :])
    values[...] = value32.astype(BF16)
    values_t[...] = value32.T.astype(BF16)

    lane_head = lax.broadcasted_iota(jnp.int32, (128, width), 1) // size

    def spread(target, field):
        for b in range(blocks):
            part = field[b * 128 : (b + 1) * 128]
            for h in range(heads):
                target[b, h * 128 : (h + 1) * 128, :] = jnp.where(lane_head == h, part, 0.0).astype(BF16)

    own = frame_ref[...]
    spread(stack_q, nn(own, wqkv_ref[:, :width]).astype(BF16).astype(F32))

    at_key = lax.broadcasted_iota(jnp.int32, (reach, 128), 0)
    at_query = lax.broadcasted_iota(jnp.int32, (reach, 128), 1)
    key_row, key_col = at_key // across, at_key % across
    key_col = jnp.where(key_col < cols + EDGE, key_col, key_col - across)
    row_gap = key_row - at_query // cols
    col_gap = key_col - at_query % cols
    near = (row_gap >= 0) & (row_gap <= 2 * RADIUS) & (col_gap >= -RADIUS) & (col_gap <= RADIUS)
    for b in range(blocks):
        row_global = key_row + (lat_first + b * block_rows - RADIUS)
        seen = near & (row_global >= 0) & (row_global < lat_total)
        bias[b] = jnp.where(seen, 0.0, negative_big)

    def diagonal(target, product, b, pair):
        at = pl.multiple_of(pair * 2 * size, 2 * size)
        lane = pl.multiple_of(b * 128, 128)
        target[pl.ds(at, size), pl.ds(lane, 128)] = product[:size, :128]
        target[pl.ds(at + size, size), pl.ds(lane, 128)] = product[size:, 128:]

    def forward(index, _):
        b, pair = index // pairs, index % pairs
        at = pl.multiple_of(pair * 256, 256)
        first = pl.multiple_of(b * step, step)
        rim_bias = bias[b]
        scores = nt(keys[pl.ds(first, reach), :], stack_q[b, pl.ds(at, 256), :]) * head_scale
        scores = scores + jnp.concatenate([rim_bias, rim_bias], axis=1)
        peak = jnp.max(scores, axis=0, keepdims=True)
        expo = jnp.exp(scores - peak)
        total = jnp.sum(expo, axis=0, keepdims=True)
        weight = expo * (1.0 / total)
        probs[index] = weight
        weight_bf = weight.astype(BF16)
        probs_bf[b, :, pl.ds(at, 256)] = weight_bf
        some = values_t[pl.ds(pl.multiple_of(pair * 2 * size, 2 * size), 2 * size), pl.ds(first, reach)]
        diagonal(att_t, nn(some, weight_bf), b, pair)
        return _

    lax.fori_loop(0, blocks * pairs, forward, 0)

    attended_t = att_t[...]
    attended = attended_t.T.astype(BF16)
    proj = nn(attended, wproj_ref[...])
    factor_one = rms_factor(proj)
    mid32 = own.astype(F32) + proj * factor_one * gain_attn_ref[...]
    mid = mid32.astype(BF16)

    downward = jnp.zeros((rows * cols, width), F32)
    for c in range(ff // 256):
        upward = nn(mid, wup_ref[:, c * 256 : (c + 1) * 256])
        activated, derivative = gelu_pair(upward)
        hidden_c = activated.astype(BF16)
        hidden[c] = activated
        slope[c] = derivative
        downward = downward + nn(hidden_c, wdown_ref[c * 256 : (c + 1) * 256, :])
    factor_two = rms_factor(downward)
    block_out_ref[...] = (mid.astype(F32) + downward * factor_two * gain_mlp_ref[...]).astype(BF16)

    incoming = cot_ref[...].astype(F32)
    gain_term = incoming * downward * factor_two
    gains_ref[side[1]] = jnp.broadcast_to(jnp.sum(gain_term.T, axis=1, keepdims=True), (width, 128))
    d_down = norm_backward(incoming * gain_mlp_ref[...], downward, factor_two).astype(BF16)
    mid_t = mid.astype(F32).T.astype(BF16)
    d_mid = incoming
    for c in range(ff // 256):
        d_up = (nt(d_down, wdown_ref[c * 256 : (c + 1) * 256, :]) * slope[c]).astype(BF16)
        d_mid = d_mid + nt(d_up, wup_ref[:, c * 256 : (c + 1) * 256])
        put(c, nn(mid_t, d_up))
        put(6 + c, nn(hidden[c].T.astype(BF16), d_down))
    d_mid_ref[...] = d_mid
    gain_term = d_mid * proj * factor_one
    gains_ref[side[0]] = jnp.broadcast_to(jnp.sum(gain_term.T, axis=1, keepdims=True), (width, 128))
    d_proj = norm_backward(d_mid * gain_attn_ref[...], proj, factor_one).astype(BF16)
    put(4, nn(attended_t.astype(BF16), d_proj))
    spread(stack_o, nt(d_proj, wproj_ref[...]).astype(BF16).astype(F32))

    def backward(index, _):
        b, pair = index // pairs, index % pairs
        at = pl.multiple_of(pair * 256, 256)
        first = pl.multiple_of(b * step, step)
        d_probs = nt(values[pl.ds(first, reach), :], stack_o[b, pl.ds(at, 256), :])
        weight = probs[index]
        d_weighted = jnp.sum(weight * d_probs, axis=0, keepdims=True)
        d_score = (weight * (d_probs - d_weighted) * head_scale).astype(BF16)
        d_scores[b, :, pl.ds(at, 256)] = d_score
        some = keys_t[pl.ds(pl.multiple_of(pair * 2 * size, 2 * size), 2 * size), pl.ds(first, reach)]
        diagonal(dq_t, nn(some, d_score), b, pair)
        return _

    lax.fori_loop(0, blocks * pairs, backward, 0)

    pair_grads[...] = jnp.zeros_like(pair_grads)
    for b in range(blocks):
        pair_grads[b * step : b * step + reach, :width] += nn(d_scores[b], stack_q[b])
        pair_grads[b * step : b * step + reach, width:] += nn(probs_bf[b], stack_o[b])

    dq = dq_t[...].T.astype(BF16)
    dq_ref[...] = dq
    up_ref[...] = pair_grads[0:rim, :].astype(BF16)
    down_ref[...] = pair_grads[rim + inner : inner + 2 * rim, :].astype(BF16)
    centre_ref[...] = pair_grads[rim : rim + inner, :]

    put(5, nn(own.astype(F32).T.astype(BF16), dq))
    grid_t = halo[...].astype(F32).T.astype(BF16)
    for half in range(2):
        terms = pair_grads[:, half * width : (half + 1) * width]
        high = terms.astype(BF16)
        low = (terms - high.astype(F32)).astype(BF16)
        put(10 + half, nn(grid_t, high) + nn(grid_t, low))


def local_part(where, frame, wide, top, bottom, weights, cotangent, dims):
    rows, cols, width, ff = dims["rows"], dims["cols"], dims["width"], dims["ff"]
    across = cols + 2 * EDGE
    grid = (rows + 2 * RADIUS) * across
    rim = RADIUS * across
    block_rows = 128 // cols
    blocks = rows // block_rows
    reach = (block_rows + 2 * RADIUS) * across
    tokens = rows * cols
    pairs = HEADS // 2
    shape = jax.ShapeDtypeStruct
    vmem = pl.BlockSpec(memory_space=pltpu.VMEM)
    outs = [
        shape((tokens, width), BF16),
        shape((tokens, width), F32),
        shape((tokens, width), BF16),
        shape((rim, 2 * width), BF16),
        shape((rim, 2 * width), BF16),
        shape((rows * across, 2 * width), F32),
        shape((2, 3072, 128), F32),
        shape((2, width, 128), F32),
    ]
    return pl.pallas_call(
        functools.partial(local_kernel, dims),
        out_shape=outs,
        in_specs=[pl.BlockSpec(memory_space=pltpu.SMEM)] + [vmem] * 11,
        out_specs=[vmem] * len(outs),
        scratch_shapes=[
            pltpu.VMEM((grid, width), BF16),
            pltpu.VMEM((grid, width), BF16),
            pltpu.VMEM((grid, width), BF16),
            pltpu.VMEM((width, grid), BF16),
            pltpu.VMEM((width, grid), BF16),
            pltpu.VMEM((blocks, HEADS * 128, width), BF16),
            pltpu.VMEM((blocks, HEADS * 128, width), BF16),
            pltpu.VMEM((blocks, reach, 128), F32),
            pltpu.VMEM((blocks * pairs, reach, 256), F32),
            pltpu.VMEM((blocks, reach, HEADS * 128), BF16),
            pltpu.VMEM((blocks, reach, HEADS * 128), BF16),
            pltpu.VMEM((width, tokens), F32),
            pltpu.VMEM((width, tokens), F32),
            pltpu.VMEM((ff // 256, tokens, 256), F32),
            pltpu.VMEM((ff // 256, tokens, 256), F32),
            pltpu.VMEM((grid, 2 * width), F32),
        ],
        name="local_part",
    )(where, frame, wide, top, bottom, *weights, cotangent)


def chip_groups(lat_n, lon_n):
    def flat(z, x, y, core):
        return (z * 2 + x // 2) * lon_n + y * 4 + x % 2 * 2 + core

    n_z, n_y = lat_n // 2, lon_n // 4
    over_x = [
        [flat(z, x, y, core) for x in range(4)] for z in range(n_z) for y in range(n_y) for core in range(2)
    ]
    over_yz = [
        [flat(z, x, y, core) for z in range(n_z) for y in range(n_y)] for x in range(4) for core in range(2)
    ]
    return over_x, over_yz


def on_device(
    frame, weight_qkv, weight_proj, gain_attn, weight_up, weight_down, gain_mlp, cotangent
):
    rows, cols, width = frame.shape
    ff = weight_up.shape[1]
    lat_n, lon_n = lax.axis_size("lat"), lax.axis_size("lon")
    tokens = rows * cols
    grad_scale = (tokens * lat_n * lon_n) ** (-0.5)
    across = cols + 2 * EDGE
    dims = {"rows": rows, "cols": cols, "width": width, "ff": ff, "lat_total": rows * lat_n}
    core = lax.axis_index("lon") % 2
    where = jnp.stack([lax.axis_index("lat") * rows, core]).astype(jnp.int32)

    east = [(i, (i + 1) % lon_n) for i in range(lon_n)]
    west = [(j, i) for i, j in east]
    south = [(i, i + 1) for i in range(lat_n - 1)]
    north = [(j, i) for i, j in south]

    from_east = lax.ppermute(frame[:, :EDGE], "lon", west)
    from_west = lax.ppermute(frame[:, cols - EDGE :], "lon", east)
    wide = jnp.concatenate([frame, from_east, from_west], axis=1)
    bottom = lax.ppermute(wide[:RADIUS], "lat", north)
    top = lax.ppermute(wide[rows - RADIUS :], "lat", south)

    weights = (
        weight_qkv,
        weight_proj,
        gain_attn.reshape(1, width),
        weight_up,
        weight_down,
        gain_mlp.reshape(1, width),
    )
    flat = (-1, width)
    block_out, d_mid, dq, up, down, centre, grads, gains = local_part(
        where,
        frame.reshape(flat),
        wide.reshape(flat),
        top.reshape(flat),
        bottom.reshape(flat),
        weights,
        cotangent.reshape(flat),
        dims,
    )

    up = lax.ppermute(up, "lat", north).reshape(RADIUS, across, 2 * width).astype(F32)
    down = lax.ppermute(down, "lat", south).reshape(RADIUS, across, 2 * width).astype(F32)
    rest = rows - RADIUS
    centre = centre.reshape(rows, across, 2 * width)
    centre = centre + jnp.pad(up, ((rest, 0), (0, 0), (0, 0))) + jnp.pad(down, ((0, rest), (0, 0), (0, 0)))
    to_east = centre[:, cols : cols + EDGE].astype(BF16)
    to_west = centre[:, cols + EDGE :].astype(BF16)
    from_west = lax.ppermute(to_east, "lon", east).astype(F32)
    from_east = lax.ppermute(to_west, "lon", west).astype(F32)
    rest = cols - EDGE
    owned = (
        centre[:, :cols]
        + jnp.pad(from_west, ((0, 0), (0, rest), (0, 0)))
        + jnp.pad(from_east, ((0, 0), (rest, 0), (0, 0)))
    )
    d_projected = jnp.concatenate([dq, owned.reshape(tokens, 2 * width).astype(BF16)], axis=1)
    grad_frame = (d_mid + nt(d_projected, weight_qkv)).astype(BF16)

    both = ("lat", "lon")
    devices = lat_n * lon_n
    swap = [(i, i ^ 1) for i in range(devices)]
    over_x, over_yz = chip_groups(lat_n, lon_n)
    n_x, n_yz = len(over_x[0]), len(over_yz[0])
    chips = n_x * n_yz

    def exchange(blocks, groups):
        return lax.all_to_all(blocks, both, 0, 0, axis_index_groups=groups)

    other, other_gain = lax.ppermute((grads[1], gains[1]), both, swap)
    held = (grads[0] + other).reshape(n_x, -1, 128)
    held_gain = (gains[0] + other_gain).reshape(n_x, -1, 128)
    n_main = held.shape[1]
    held = jnp.sum(exchange(jnp.concatenate([held, held_gain], axis=1), over_x), axis=0)
    held_gain = held[n_main:].reshape(n_yz, -1, 128)
    held = held[:n_main].reshape(n_yz, -1, 128)
    n_main = held.shape[1]
    held = jnp.sum(exchange(jnp.concatenate([held, held_gain], axis=1), over_yz), axis=0) * grad_scale
    body = held[:n_main].astype(BF16)
    gain = held[n_main:]
    high = gain.astype(BF16)
    low = (gain - high.astype(F32)).astype(BF16)
    mine = jnp.concatenate([body, high, low], axis=0)
    n_rows = mine.shape[0]
    mine = mine.reshape(1, -1, 2, 128)
    mine = exchange(jnp.broadcast_to(mine, (n_yz,) + mine.shape[1:]), over_yz)
    mine = mine.reshape((1,) + mine.shape)
    mine = exchange(jnp.broadcast_to(mine, (n_x,) + mine.shape[1:]), over_x)
    theirs = lax.ppermute(mine, both, swap)
    first = jnp.where(core == 0, mine, theirs)
    second = jnp.where(core == 0, theirs, mine)

    def unpack(field):
        flat_rows = field.reshape(chips, n_rows, 128)
        blocks = flat_rows[:, :n_main].reshape(6, 2, 256, 128)
        tail = flat_rows[:, n_main:, 0].astype(F32).reshape(chips, 2, -1)
        return blocks, (tail[:, 0] + tail[:, 1]).reshape(-1)

    first, sum_gain_attn = unpack(first)
    second, sum_gain_mlp = unpack(second)

    def beside(blocks):
        return blocks.transpose(2, 0, 1, 3).reshape(256, -1)

    return (
        block_out.reshape(rows, cols, width),
        grad_frame.reshape(rows, cols, width),
        beside(jnp.concatenate([first[5:6], second[4:6]], axis=0)),
        beside(first[4:5]),
        beside(first[:4]),
        second[:4].transpose(0, 2, 1, 3).reshape(ff, width),
        sum_gain_attn,
        sum_gain_mlp,
    )


def solution(mesh):
    return jax.shard_map(
        on_device,
        mesh=mesh,
        in_specs=(P("lat", "lon", None), P(), P(), P(), P(), P(), P(), P("lat", "lon", None)),
        out_specs=(P("lat", "lon", None), P("lat", "lon", None), P(), P(), P(), P(), P(), P()),
        check_vma=False,
    )
```

time: 707 us -> 183 us (0.26); the launches traced: 695 us -> 181 us
  local copies, waits for them, and re-layouts: 249 us -> 12.7 us
  waiting for transfers between devices: 200 us -> 15.2 us
  matrix products: 58.8 us -> 1.37 us
  blocking collectives: 107 us -> 75.6 us
  other arithmetic: 31.2 us -> 6.05 us
  Pallas kernels: 0 us -> 20.7 us
  starting transfers between devices: 33.9 us -> 48.5 us
  between operations: 15.2 us -> 1.12 us
    psum x1 -> x0, waiting for transfers between devices: 184 us -> none  [on_device(): lax.psum((local_qkv, local_proj, local_up, local_down, local_gain_attn, l...]
    reshape x11 -> x3, local copies, waits for them, and re-layouts: 115 us -> 0.4 us  [the longest x2 0.36 us: unpack(): blocks = flat_rows[:, :n_main].reshape(6, 2, 256, 128)]
    psum x1 -> x0, blocking collectives: 107 us -> none  [on_device(): lax.psum((local_qkv, local_proj, local_up, local_down, local_gain_attn, l...]
    all_to_all x0 -> x3, blocking collectives: none -> 75.6 us  [exchange(): return lax.all_to_all(blocks, both, 0, 0, axis_index_groups=groups)]
    dot_general x18 -> x1, matrix products: 58.8 us -> 1.37 us  [nt(): lax.dot_general(left, right, (((1,), (1,)), ((), ())), preferred_element_...]
    transpose x3 -> x7, local copies, waits for them, and re-layouts: 40.8 us -> 1.14 us  [the longest x2 0.58 us: on_device(): second[:4].transpose(0, 2, 1, 3).reshape(ff, width)]
    another operation x29 -> x0, local copies, waits for them, and re-layouts: 29.1 us -> none  [the longest x28 29 us: row_strips(): jnp.stack([lax.slice_in_dim(padded, offset, offset + rows, axis=0) for of...]
    unnamed x112 -> x26, local copies, waits for them, and re-layouts: 33.7 us -> 5.22 us
  transfers between devices with their start and end apart: 9 -> 12, of which waited for: 6 -> 6; matrix products, arithmetic and copies ran while one was open for 1% -> 3% of each run, Pallas kernels for 0% -> 0%
where the time goes in v1:
time: 183 us; the launch traced here: 181 us
  blocking collectives  75.6 us (41%)
  starting transfers between devices  48.5 us (27%)
  Pallas kernels  20.7 us (11%)
  waiting for transfers between devices  15.2 us (8%)
  local copies, waits for them, and re-layouts  12.7 us (7%)
  other arithmetic  6.05 us (3%)
    all_to_all x3, blocking collectives, exchange(): return lax.all_to_all(blocks, both, 0, 0, axis_index_groups=groups)  75.6 us
    pallas_call x1, Pallas kernels, local_part(): pl.pallas_call(functools.partial(local_kernel, dims), out_shape=outs, in_...  20.7 us
    ppermute x2, starting transfers between devices, on_device(): other, other_gain = lax.ppermute((grads[1], gains[1]), both, swap)  9.73 us
    ppermute x1, waiting for transfers between devices, on_device(): lax.ppermute(up, 'lat', north).reshape(RADIUS, across, 2 * width)  7.96 us
    ppermute x1, starting transfers between devices, on_device(): from_east = lax.ppermute(frame[:, :EDGE], 'lon', west)  6.17 us
    ppermute x1, starting transfers between devices, on_device(): theirs = lax.ppermute(mine, both, swap)  5.67 us
    ppermute x1, starting transfers between devices, on_device(): lax.ppermute(down, 'lat', south).reshape(RADIUS, across, 2 * width)  5.5 us
    ppermute x1, starting transfers between devices, on_device(): top = lax.ppermute(wide[rows - RADIUS:], 'lat', south)  5.5 us
  transfers between devices with their start and end apart: 12, of which 6 were waited for; matrix products, arithmetic and copies ran while one was open for 3% of the time, Pallas kernels for 0%

profile of v1, /device:TPU:1, one launch (start us, length us, event | category | flops | bytes accessed | tf_op | source)
XLA Modules:
  0.0 181.2 jit_solution(18168227968214048004)
XLA Ops:
  1.5 4.5 %collective-permute-start.1 = (bf16[16,8,256]{2,1,0:T(8,128)(2,1)S(1)}, bf16[16,8,256]{2,1,0:T(8,128)(2,1)S(1)}, u32[]{:S(2)}, u32[]{:S(2)}) collective-permute-start(bf16[16,8,256]{2,1,0:T(8,128)(2,1)S(1)} %get-tuple-element.50), channel_id=1, source_target_pairs={{0,1},{1,2},{2,3},{3,4},{4,5},{5,6},{6,7},{7,8},{8,9},{9,10},{10,1... | collective-permute-start | bytes 196616 | tf_op jit(solution)/shard_map/ppermute | solution.py:321
  6.0 6.2 %collective-permute-start = (bf16[16,8,256]{2,1,0:T(8,128)(2,1)S(1)}, bf16[16,8,256]{2,1,0:T(8,128)(2,1)S(1)}, u32[]{:S(2)}, u32[]{:S(2)}) collective-permute-start(bf16[16,8,256]{2,1,0:T(8,128)(2,1)S(1)} %get-tuple-element.51), channel_id=1, source_target_pairs={{1,0},{2,1},{3,2},{4,3},{5,4},{6,5},{7,6},{8,7},{9,8},{10,9},{11,1... | collective-permute-start | bytes 196616 | tf_op jit(solution)/shard_map/ppermute | solution.py:320
  13.2 1.3 collective-permute-start.3
  14.5 5.5 %collective-permute-start.2 = (bf16[6,32,256]{2,1,0:T(8,128)(2,1)S(1)}, bf16[6,32,256]{2,1,0:T(8,128)(2,1)S(1)}, u32[]{:S(2)}, u32[]{:S(2)}) collective-permute-start(bf16[6,32,256]{2,1,0:T(8,128)(2,1)S(1)} %get-tuple-element.49), channel_id=1, source_target_pairs={{0,32},{32,64},{64,96},{96,128},{128,160},{160,192},{192,224},{224... | collective-permute-start | bytes 294920 | tf_op jit(solution)/shard_map/ppermute | solution.py:324
  22.3 20.7 %local_part.1 = (bf16[256,256]{1,0:T(8,128)(2,1)}, f32[256,256]{1,0:T(8,128)}, bf16[256,256]{1,0:T(8,128)(2,1)}, bf16[192,512]{1,0:T(8,128)(2,1)}, bf16[192,512]...) custom-call(s32[2]{0:T(128)} %pad_add_fusion.where_ref, ...), custom_call_target="tpu_custom_call" | custom-call | tf_op jit(solution)/shard_map/local_part/pallas_call | solution.py:261
  43.0 1.7 slice_bitcast_fusion
  44.6 7.8 %collective-permute-start.8 = (f32[3072,128]{1,0:T(8,128)S(1)}, f32[3072,128]{1,0:T(8,128)S(1)}, u32[]{:S(2)}, u32[]{:S(2)}) collective-permute-start(f32[3072,128]{1,0:T(8,128)S(1)} %slice_bitcast_fusion), channel_id=1, source_target_pairs={{0,1},{1,0},{2,3},{3,2},{4,5},{5,4},{6,7},{7,6},{8,9},{9,8},{10,11... | collective-permute-start | bytes 4718600 | tf_op jit(solution)/shard_map/ppermute | solution.py:374
  52.5 1.9 %collective-permute-start.9 = (f32[256,128]{1,0:T(8,128)S(1)}, f32[256,128]{1,0:T(8,128)S(1)}, u32[]{:S(2)}, u32[]{:S(2)}) collective-permute-start(f32[256,128]{1,0:T(8,128)S(1)} %slice_bitcast_fusion.4), channel_id=1, source_target_pairs={{0,1},{1,0},{2,3},{3,2},{4,5},{5,4},{6,7},{7,6},{8,9},{9,8},{10,11... | collective-permute-start | bytes 393224 | tf_op jit(solution)/shard_map/ppermute | solution.py:374
  54.4 1.3 collective-permute-done.9
  56.0 26.3 %all_to_all.20 = f32[4,832,128]{2,1,0:T(8,128)S(1)} all-to-all(f32[4,832,128]{2,1,0:T(8,128)S(1)} %pad_maximum_fusion), channel_id=1, replica_groups={{0,2,32,34},{1,3,33,35},{4,6,36,38},{5,7,37,39},{8,10,40,42},{9,11,41,4..., dimensions={0} | all-to-all | bytes 3407872 | tf_op jit(solution)/shard_map/all_to_all | solution.py:372
  82.7 30.0 %all_to_all.21 = f32[64,13,128]{2,1,0:T(8,128)S(1)} all-to-all(f32[64,13,128]{2,1,0:T(8,128)S(1)} %pad_maximum_fusion.1), channel_id=1, replica_groups={{0,4,8,12,16,20,24,28,64,68,72,76,80,84,88,92,128,132,136,140,144,148,1..., dimensions={0} | all-to-all | bytes 851968 | tf_op jit(solution)/shard_map/all_to_all | solution.py:372
  112.9 19.2 %all_to_all.22 = bf16[64,7,2,128]{3,2,1,0:T(2,128)(2,1)S(1)} all-to-all(bf16[64,7,2,128]{3,2,1,0:T(2,128)(2,1)S(1)} %broadcast_in_dim.13), channel_id=1, replica_groups={{0,4,8,12,16,20,24,28,64,68,72,76,80,84,88,92,128,132,136,140,144,148,1..., dimensions={0} | all-to-all | bytes 458752 | tf_op jit(solution)/shard_map/all_to_all | solution.py:372
  132.2 1.2 broadcast_in_dim.14
  133.4 3.5 %all-to-all-start.3 = ((bf16[4,64,7,2,128]{4,1,3,2,0:T(8,128)(2,1)}), bf16[4,64,7,2,128]{4,1,3,2,0:T(8,128)(2,1)S(1)}, u32[]{:S(2)}, u32[]{:S(2)}) async-start(bf16[4,64,7,2,128]{4,1,3,2,0:T(8,128)(2,1)} %broadcast_in_dim.14), calls=%async_computation.3 | async-start | bytes 1835008 | tf_op jit(solution)/shard_map/all_to_all | solution.py:372
  136.9 1.3 collective-permute-start.4
  138.2 5.5 %collective-permute-start.5 = (bf16[192,512]{1,0:T(8,128)(2,1)S(1)}, bf16[192,512]{1,0:T(8,128)(2,1)S(1)}, u32[]{:S(2)}, u32[]{:S(2)}) collective-permute-start(bf16[192,512]{1,0:T(8,128)(2,1)S(1)} %copy-done.8), channel_id=1, source_target_pairs={{0,32},{32,64},{64,96},{96,128},{128,160},{160,192},{192,224},{224... | collective-permute-start | bytes 589832 | tf_op jit(solution)/shard_map/ppermute | solution.py:347
  143.7 8.0 %collective-permute-done.4 = bf16[192,512]{1,0:T(8,128)(2,1)S(1)} collective-permute-done((bf16[192,512]{1,0:T(8,128)(2,1)S(1)}, bf16[192,512]{1,0:T(8,128)(2,1)S(1)}, u32[]{:S(2)}, u32[]{:S(2)}) %collective-permute-start.4) | collective-permute-done | bytes 196640 | tf_op jit(solution)/shard_map/ppermute | solution.py:346
  152.8 5.7 %collective-permute-start.10 = (bf16[4,64,7,2,128]{4,1,0,3,2:T(8,128)(2,1)S(1)}, bf16[4,64,7,2,128]{4,1,0,3,2:T(8,128)(2,1)}, u32[]{:S(2)}, u32[]{:S(2)}) collective-permute-start(bf16[4,64,7,2,128]{4,1,0,3,2:T(8,128)(2,1)S(1)} %copy.32), channel_id=1, source_target_pairs={{0,1},{1,0},{2,3},{3,2},{4,5},{5,4},{6,7},{7,6},{8,9},{9,8},{10,11... | collective-permute-start | bytes 2752520 | tf_op jit(solution)/shard_map/ppermute | solution.py:393
  159.2 3.3 %collective-permute-start.6 = (bf16[16,8,512]{2,1,0:T(8,128)(2,1)}, bf16[16,8,512]{2,1,0:T(8,128)(2,1)S(1)}, u32[]{:S(2)}, u32[]{:S(2)}) collective-permute-start(bf16[16,8,512]{2,1,0:T(8,128)(2,1)} %get-tuple-element.46), channel_id=1, source_target_pairs={{0,1},{1,2},{2,3},{3,4},{4,5},{5,6},{6,7},{7,8},{8,9},{9,10},{10,1... | collective-permute-start | bytes 393224 | tf_op jit(solution)/shard_map/ppermute | solution.py:353
  162.4 2.1 %collective-permute-start.7 = (bf16[16,8,512]{2,1,0:T(8,128)(2,1)S(1)}, bf16[16,8,512]{2,1,0:T(8,128)(2,1)S(1)}, u32[]{:S(2)}, u32[]{:S(2)}) collective-permute-start(bf16[16,8,512]{2,1,0:T(8,128)(2,1)S(1)} %get-tuple-element.47), channel_id=1, source_target_pairs={{1,0},{2,1},{3,2},{4,3},{5,4},{6,5},{7,6},{8,7},{9,8},{10,9},{11,1... | collective-permute-start | bytes 393224 | tf_op jit(solution)/shard_map/ppermute | solution.py:354
  164.7 4.0 %collective-permute-done.7 = bf16[16,8,512]{2,1,0:T(8,128)(2,1)S(1)} collective-permute-done((bf16[16,8,512]{2,1,0:T(8,128)(2,1)S(1)}, bf16[16,8,512]{2,1,0:T(8,128)(2,1)S(1)}, u32[]{:S(2)}, u32[]{:S(2)}) %collective-permute-start.7) | collective-permute-done | bytes 131104 | tf_op jit(solution)/shard_map/ppermute | solution.py:354
  168.8 1.4 fusion.2
  170.2 1.6 add_convert_fusion
  171.8 1.3 broadcast_select_fusion.1
  (80 shorter events, 14.8 us)
Async XLA Ops:
  1.5 11.6 %collective-permute-start.1 = (bf16[16,8,256]{2,1,0:T(8,128)(2,1)S(1)}, bf16[16,8,256]{2,1,0:T(8,128)(2,1)S(1)}, u32[]{:S(2)}, u32[]{:S(2)}) collective-permute-start(bf16[16,8,256]{2,1,0:T(8,128)(2,1)S(1)} %get-tuple-element.50), channel_id=1, source_target_pairs={{0,1},{1,2},{2,3},{3,4},{4,5},{5,6},{6,7},{7,8},{8,9},{9,10},{10,1... | collective-permute-start | bytes 196616 | tf_op jit(solution)/shard_map/ppermute | solution.py:321
  6.0 7.1 %collective-permute-start = (bf16[16,8,256]{2,1,0:T(8,128)(2,1)S(1)}, bf16[16,8,256]{2,1,0:T(8,128)(2,1)S(1)}, u32[]{:S(2)}, u32[]{:S(2)}) collective-permute-start(bf16[16,8,256]{2,1,0:T(8,128)(2,1)S(1)} %get-tuple-element.51), channel_id=1, source_target_pairs={{1,0},{2,1},{3,2},{4,3},{5,4},{6,5},{7,6},{8,7},{9,8},{10,9},{11,1... | collective-permute-start | bytes 196616 | tf_op jit(solution)/shard_map/ppermute | solution.py:320
  13.2 8.5 %copy-start.2 = (bf16[16,32,256]{2,1,0:T(8,128)(2,1)}, bf16[16,32,256]{2,1,0:T(8,128)(2,1)S(1)}, u32[]{:S(2)}) copy-start(bf16[16,32,256]{2,1,0:T(8,128)(2,1)S(1)} %constant_dynamic-update-slice_fusion) | copy-start | bytes 786436
  13.2 7.5 %collective-permute-start.3 = (bf16[6,32,256]{2,1,0:T(8,128)(2,1)S(1)}, bf16[6,32,256]{2,1,0:T(8,128)(2,1)S(1)}, u32[]{:S(2)}, u32[]{:S(2)}) collective-permute-start(bf16[6,32,256]{2,1,0:T(8,128)(2,1)S(1)} %get-tuple-element.48), channel_id=1, source_target_pairs={{32,0},{64,32},{96,64},{128,96},{160,128},{192,160},{224,192},{256... | collective-permute-start | bytes 294920 | tf_op jit(solution)/shard_map/ppermute | solution.py:323
  14.5 7.1 %collective-permute-start.2 = (bf16[6,32,256]{2,1,0:T(8,128)(2,1)S(1)}, bf16[6,32,256]{2,1,0:T(8,128)(2,1)S(1)}, u32[]{:S(2)}, u32[]{:S(2)}) collective-permute-start(bf16[6,32,256]{2,1,0:T(8,128)(2,1)S(1)} %get-tuple-element.49), channel_id=1, source_target_pairs={{0,32},{32,64},{64,96},{96,128},{128,160},{160,192},{192,224},{224... | collective-permute-start | bytes 294920 | tf_op jit(solution)/shard_map/ppermute | solution.py:324
  20.7 1.0 copy-start.6
  21.6 0.6 copy-start.7
  42.9 9.5 %copy-start.5 = (f32[2,256,128]{2,1,0:T(8,128)S(1)}, f32[2,256,128]{2,1,0:T(8,128)}, u32[]{:S(2)}) copy-start(f32[2,256,128]{2,1,0:T(8,128)} %get-tuple-element.23) | copy-start | bytes 786436
  42.9 12.8 %copy-start.1 = (f32[2,3072,128]{2,1,0:T(8,128)S(1)}, f32[2,3072,128]{2,1,0:T(8,128)}, u32[]{:S(2)}) copy-start(f32[2,3072,128]{2,1,0:T(8,128)} %get-tuple-element.22) | copy-start | bytes 9437188
  44.6 11.1 %collective-permute-start.8 = (f32[3072,128]{1,0:T(8,128)S(1)}, f32[3072,128]{1,0:T(8,128)S(1)}, u32[]{:S(2)}, u32[]{:S(2)}) collective-permute-start(f32[3072,128]{1,0:T(8,128)S(1)} %slice_bitcast_fusion), channel_id=1, source_target_pairs={{0,1},{1,0},{2,3},{3,2},{4,5},{5,4},{6,7},{7,6},{8,9},{9,8},{10,11... | collective-permute-start | bytes 4718600 | tf_op jit(solution)/shard_map/ppermute | solution.py:374
  52.5 3.2 %collective-permute-start.9 = (f32[256,128]{1,0:T(8,128)S(1)}, f32[256,128]{1,0:T(8,128)S(1)}, u32[]{:S(2)}, u32[]{:S(2)}) collective-permute-start(f32[256,128]{1,0:T(8,128)S(1)} %slice_bitcast_fusion.4), channel_id=1, source_target_pairs={{0,1},{1,0},{2,3},{3,2},{4,5},{5,4},{6,7},{7,6},{8,9},{9,8},{10,11... | collective-permute-start | bytes 393224 | tf_op jit(solution)/shard_map/ppermute | solution.py:374
  132.2 4.7 %copy-start.9 = (bf16[192,512]{1,0:T(8,128)(2,1)S(1)}, bf16[192,512]{1,0:T(8,128)(2,1)}, u32[]{:S(2)}) copy-start(bf16[192,512]{1,0:T(8,128)(2,1)} %get-tuple-element.20) | copy-start | bytes 589828
  132.2 6.0 %copy-start.8 = (bf16[192,512]{1,0:T(8,128)(2,1)S(1)}, bf16[192,512]{1,0:T(8,128)(2,1)}, u32[]{:S(2)}) copy-start(bf16[192,512]{1,0:T(8,128)(2,1)} %get-tuple-element.21) | copy-start | bytes 589828
  132.2 20.3 %copy-start.3 = (f32[512,512]{1,0:T(8,128)S(1)}, f32[512,512]{1,0:T(8,128)}, u32[]{:S(2)}) copy-start(f32[512,512]{1,0:T(8,128)} %get-tuple-element.19) | copy-start | bytes 3145732
  133.4 19.3 %all-to-all-start.3 = ((bf16[4,64,7,2,128]{4,1,3,2,0:T(8,128)(2,1)}), bf16[4,64,7,2,128]{4,1,3,2,0:T(8,128)(2,1)S(1)}, u32[]{:S(2)}, u32[]{:S(2)}) async-start(bf16[4,64,7,2,128]{4,1,3,2,0:T(8,128)(2,1)} %broadcast_in_dim.14), calls=%async_computation.3 | async-start | bytes 1835008 | tf_op jit(solution)/shard_map/all_to_all | solution.py:372
  136.9 14.8 %collective-permute-start.4 = (bf16[192,512]{1,0:T(8,128)(2,1)S(1)}, bf16[192,512]{1,0:T(8,128)(2,1)S(1)}, u32[]{:S(2)}, u32[]{:S(2)}) collective-permute-start(bf16[192,512]{1,0:T(8,128)(2,1)S(1)} %copy-done.9), channel_id=1, source_target_pairs={{32,0},{64,32},{96,64},{128,96},{160,128},{192,160},{224,192},{256... | collective-permute-start | bytes 589832 | tf_op jit(solution)/shard_map/ppermute | solution.py:346
  138.2 14.3 %collective-permute-start.5 = (bf16[192,512]{1,0:T(8,128)(2,1)S(1)}, bf16[192,512]{1,0:T(8,128)(2,1)S(1)}, u32[]{:S(2)}, u32[]{:S(2)}) collective-permute-start(bf16[192,512]{1,0:T(8,128)(2,1)S(1)} %copy-done.8), channel_id=1, source_target_pairs={{0,32},{32,64},{64,96},{96,128},{128,160},{160,192},{192,224},{224... | collective-permute-start | bytes 589832 | tf_op jit(solution)/shard_map/ppermute | solution.py:347
  152.8 19.0 %collective-permute-start.10 = (bf16[4,64,7,2,128]{4,1,0,3,2:T(8,128)(2,1)S(1)}, bf16[4,64,7,2,128]{4,1,0,3,2:T(8,128)(2,1)}, u32[]{:S(2)}, u32[]{:S(2)}) collective-permute-start(bf16[4,64,7,2,128]{4,1,0,3,2:T(8,128)(2,1)S(1)} %copy.32), channel_id=1, source_target_pairs={{0,1},{1,0},{2,3},{3,2},{4,5},{5,4},{6,7},{7,6},{8,9},{9,8},{10,11... | collective-permute-start | bytes 2752520 | tf_op jit(solution)/shard_map/ppermute | solution.py:393
  159.2 5.5 %collective-permute-start.6 = (bf16[16,8,512]{2,1,0:T(8,128)(2,1)}, bf16[16,8,512]{2,1,0:T(8,128)(2,1)S(1)}, u32[]{:S(2)}, u32[]{:S(2)}) collective-permute-start(bf16[16,8,512]{2,1,0:T(8,128)(2,1)} %get-tuple-element.46), channel_id=1, source_target_pairs={{0,1},{1,2},{2,3},{3,4},{4,5},{5,6},{6,7},{7,8},{8,9},{9,10},{10,1... | collective-permute-start | bytes 393224 | tf_op jit(solution)/shard_map/ppermute | solution.py:353
  162.4 6.3 %collective-permute-start.7 = (bf16[16,8,512]{2,1,0:T(8,128)(2,1)S(1)}, bf16[16,8,512]{2,1,0:T(8,128)(2,1)S(1)}, u32[]{:S(2)}, u32[]{:S(2)}) collective-permute-start(bf16[16,8,512]{2,1,0:T(8,128)(2,1)S(1)} %get-tuple-element.47), channel_id=1, source_target_pairs={{1,0},{2,1},{3,2},{4,3},{5,4},{6,5},{7,6},{8,7},{9,8},{10,9},{11,1... | collective-permute-start | bytes 393224 | tf_op jit(solution)/shard_map/ppermute | solution.py:354
  174.0 1.0 copy-start
  176.3 3.0 %slice-start = ((bf16[6,2,256,128]{3,2,1,0:T(8,128)(2,1)}), bf16[2,2,256,128]{3,2,1,0:T(8,128)(2,1)S(1)}, s32[]{:S(2)}) async-start(bf16[6,2,256,128]{3,2,1,0:T(8,128)(2,1)} %copy-done), calls=%async_computation.4 | async-start | bytes 524288 | tf_op jit(solution)/shard_map/slice | solution.py:412
  178.4 2.0 %copy-start.4 = (f32[256,2,1]{2,0,1:T(8,128)S(1)}, f32[256,2,1]{2,0,1:T(8,128)}, u32[]{:S(2)}) copy-start(f32[256,2,1]{2,0,1:T(8,128)} %slice_convert_fusion.1) | copy-start | bytes 6148

commit v2 on v1

--- a/solution.py
+++ b/solution.py
@@ -66,8 +66,9 @@
     up_ref,
     down_ref,
     centre_ref,
+    keep_ref,
+    send_ref,
     grads_ref,
-    gains_ref,
     halo,
     keys,
     values,
@@ -103,6 +104,10 @@
         grads_ref[side[half], row * 512 : row * 512 + 256, :] = value[:, :128]
         grads_ref[side[half], row * 512 + 256 : row * 512 + 512, :] = value[:, 128:]
 
+    def put_gain(half, terms):
+        column = jnp.sum(terms.T, axis=1, keepdims=True)
+        grads_ref[side[half], 3072:, :] = jnp.broadcast_to(column, (width, 128))
+
     rim = RADIUS * across
     inner = rows * across
     halo[0:rim, :] = top_ref[...]
@@ -184,8 +189,7 @@
     block_out_ref[...] = (mid.astype(F32) + downward * factor_two * gain_mlp_ref[...]).astype(BF16)
 
     incoming = cot_ref[...].astype(F32)
-    gain_term = incoming * downward * factor_two
-    gains_ref[side[1]] = jnp.broadcast_to(jnp.sum(gain_term.T, axis=1, keepdims=True), (width, 128))
+    put_gain(1, incoming * downward * factor_two)
     d_down = norm_backward(incoming * gain_mlp_ref[...], downward, factor_two).astype(BF16)
     mid_t = mid.astype(F32).T.astype(BF16)
     d_mid = incoming
@@ -195,8 +199,7 @@
         put(c, nn(mid_t, d_up))
         put(6 + c, nn(hidden[c].T.astype(BF16), d_down))
     d_mid_ref[...] = d_mid
-    gain_term = d_mid * proj * factor_one
-    gains_ref[side[0]] = jnp.broadcast_to(jnp.sum(gain_term.T, axis=1, keepdims=True), (width, 128))
+    put_gain(0, d_mid * proj * factor_one)
     d_proj = norm_backward(d_mid * gain_attn_ref[...], proj, factor_one).astype(BF16)
     put(4, nn(attended_t.astype(BF16), d_proj))
     spread(stack_o, nt(d_proj, wproj_ref[...]).astype(BF16).astype(F32))
@@ -234,6 +237,8 @@
         high = terms.astype(BF16)
         low = (terms - high.astype(F32)).astype(BF16)
         put(10 + half, nn(grid_t, high) + nn(grid_t, low))
+    keep_ref[...] = grads_ref[0]
+    send_ref[...] = grads_ref[1]
 
 
 def local_part(where, frame, wide, top, bottom, weights, cotangent, dims):
@@ -255,8 +260,8 @@
         shape((rim, 2 * width), BF16),
         shape((rim, 2 * width), BF16),
         shape((rows * across, 2 * width), F32),
-        shape((2, 3072, 128), F32),
-        shape((2, width, 128), F32),
+        shape((3072 + width, 128), F32),
+        shape((3072 + width, 128), F32),
     ]
     return pl.pallas_call(
         functools.partial(local_kernel, dims),
@@ -264,6 +269,7 @@
         in_specs=[pl.BlockSpec(memory_space=pltpu.SMEM)] + [vmem] * 11,
         out_specs=[vmem] * len(outs),
         scratch_shapes=[
+            pltpu.VMEM((2, 3072 + width, 128), F32),
             pltpu.VMEM((grid, width), BF16),
             pltpu.VMEM((grid, width), BF16),
             pltpu.VMEM((grid, width), BF16),
@@ -285,6 +291,98 @@
     )(where, frame, wide, top, bottom, *weights, cotangent)
 
 
+def small_kernel(body, name, outs, *args):
+    vmem = pl.BlockSpec(memory_space=pltpu.VMEM)
+    smem = pl.BlockSpec(memory_space=pltpu.SMEM)
+    return pl.pallas_call(
+        body,
+        out_shape=outs,
+        in_specs=[smem if a.dtype == jnp.int32 else vmem for a in args],
+        out_specs=jax.tree.map(lambda _: vmem, outs),
+        name=name,
+    )(*args)
+
+
+def first_rows(shape):
+    return lax.broadcasted_iota(jnp.int32, shape, 1)
+
+
+def pack_chunks(n, parts_ref, chunks_ref):
+    total = parts_ref[0]
+    for k in range(1, parts_ref.shape[0]):
+        total = total + parts_ref[k]
+    deep = 512 // n
+    chunks_ref[:, :deep] = total[:512].reshape(n, deep, 128)
+    half = n // 2
+    tail = total[512:768].reshape(half, deep, 128)
+    gain = total[768:].reshape(n, -1, 128)[:, :1]
+    row = first_rows(tail.shape)
+    for i in range(2):
+        piece = tail if i == 0 else pltpu.roll(tail, deep // 2, 1)
+        mine = gain[i * half : (i + 1) * half]
+        chunks_ref[i * half : (i + 1) * half, deep:] = jnp.where(row < deep // 2, piece, mine)
+
+
+def finish_chunk(scale, chunks_ref, own_ref):
+    n, deep = chunks_ref.shape[0], chunks_ref.shape[1] // 2
+    total = jnp.sum(chunks_ref[...], axis=0) * scale
+    high = total.astype(BF16).astype(F32)
+    row = lax.broadcasted_iota(jnp.int32, total.shape, 0)
+    total = jnp.where(row == total.shape[0] - 1, total - high, total).astype(BF16)
+    own_ref[...] = jnp.broadcast_to(total[None], (n,) + total.shape)
+
+
+def join_chunks(chunks_ref, rows_ref):
+    n, deep = chunks_ref.shape[0], chunks_ref.shape[1] // 2
+    half = n // 2
+    chunks = chunks_ref[...].astype(F32)
+    body = chunks[:, :deep].reshape(512, 128).astype(BF16)
+    tail = chunks[:, deep:]
+    row = first_rows((half, deep, 128))
+    low = jnp.where(row < deep // 2, tail[:half], pltpu.roll(tail[half:], deep // 2, 1))
+    low = low.reshape(256, 128).astype(BF16)
+    high_gain = tail[:, deep - 2].T[:16]
+    low_gain = tail[:, deep - 1].T[:16]
+    gain = jnp.concatenate([high_gain, low_gain], axis=1).astype(BF16)
+    for k in range(rows_ref.shape[0]):
+        rows_ref[k, :512] = body
+        rows_ref[k, 512:768] = low
+        rows_ref[k, 768:] = gain
+
+
+def unpack(where_ref, mine_ref, theirs_ref, qkv_ref, proj_ref, up_ref, down_ref, gain_attn_ref, gain_mlp_ref):
+    def place(half, rows_ref, gain_ref):
+        for piece in range(12):
+            k, at = divmod(piece, 3)
+            value = rows_ref[k, at * 256 : (at + 1) * 256, :]
+            block, right = divmod(piece, 2)
+            if half == 1 and block < 4:
+                down_ref[block * 256 : (block + 1) * 256, right * 128 : (right + 1) * 128] = value
+                continue
+            target, column = up_ref, block
+            if half == 1:
+                target, column = qkv_ref, block - 3
+            elif block == 4:
+                target, column = proj_ref, 0
+            elif block == 5:
+                target, column = qkv_ref, 0
+            lane = column * 256 + right * 128
+            target[:, lane : lane + 128] = value
+        for k in range(rows_ref.shape[0]):
+            gain = rows_ref[k, 768:, :].astype(F32)
+            gain_ref[k : k + 1, :] = (gain + pltpu.roll(gain, 64, 1))[:1]
+
+    @pl.when(where_ref[1] == 0)
+    def _():
+        place(0, mine_ref, gain_attn_ref)
+        place(1, theirs_ref, gain_mlp_ref)
+
+    @pl.when(where_ref[1] == 1)
+    def _():
+        place(1, mine_ref, gain_mlp_ref)
+        place(0, theirs_ref, gain_attn_ref)
+
+
 def chip_groups(lat_n, lon_n):
     def flat(z, x, y, core):
         return (z * 2 + x // 2) * lon_n + y * 4 + x % 2 * 2 + core
@@ -332,7 +430,7 @@
         gain_mlp.reshape(1, width),
     )
     flat = (-1, width)
-    block_out, d_mid, dq, up, down, centre, grads, gains = local_part(
+    block_out, d_mid, dq, up, down, centre, keep, send = local_part(
         where,
         frame.reshape(flat),
         wide.reshape(flat),
@@ -343,78 +441,79 @@
         dims,
     )
 
-    up = lax.ppermute(up, "lat", north).reshape(RADIUS, across, 2 * width).astype(F32)
-    down = lax.ppermute(down, "lat", south).reshape(RADIUS, across, 2 * width).astype(F32)
+    both = ("lat", "lon")
+    devices = lat_n * lon_n
+    swap = [(i, i ^ 1) for i in range(devices)]
+    over_x, over_yz = chip_groups(lat_n, lon_n)
+    n_x, n_yz = len(over_x[0]), len(over_yz[0])
+    shape = jax.ShapeDtypeStruct
+
+    def exchange(blocks, groups):
+        return lax.all_to_all(blocks, both, 0, 0, axis_index_groups=groups)
+
+    up = lax.ppermute(up, "lat", north)
+    down = lax.ppermute(down, "lat", south)
+
+    other = lax.ppermute(send, both, swap)
+    pieces = (keep[:3072] + other[:3072]).reshape(n_x, 768, 128)
+    tails = (keep[3072:] + other[3072:]).reshape(n_x, -1, 128)
+    parts = exchange(jnp.concatenate([pieces, tails], axis=1), over_x)
+    parts, up, down = lax.optimization_barrier((parts, up, down))
+
+    up = up.reshape(RADIUS, across, 2 * width).astype(F32)
+    down = down.reshape(RADIUS, across, 2 * width).astype(F32)
     rest = rows - RADIUS
     centre = centre.reshape(rows, across, 2 * width)
     centre = centre + jnp.pad(up, ((rest, 0), (0, 0), (0, 0))) + jnp.pad(down, ((0, rest), (0, 0), (0, 0)))
     to_east = centre[:, cols : cols + EDGE].astype(BF16)
     to_west = centre[:, cols + EDGE :].astype(BF16)
-    from_west = lax.ppermute(to_east, "lon", east).astype(F32)
-    from_east = lax.ppermute(to_west, "lon", west).astype(F32)
+    from_west = lax.ppermute(to_east, "lon", east)
+    from_east = lax.ppermute(to_west, "lon", west)
+
+    deep = 2 * 512 // n_yz
+    chunks = small_kernel(
+        functools.partial(pack_chunks, n_yz), "pack_chunks", shape((n_yz, deep, 128), F32), parts
+    )
+    chunks = exchange(chunks, over_yz)
+    chunks, from_west, from_east = lax.optimization_barrier((chunks, from_west, from_east))
+
     rest = cols - EDGE
     owned = (
         centre[:, :cols]
-        + jnp.pad(from_west, ((0, 0), (0, rest), (0, 0)))
-        + jnp.pad(from_east, ((0, 0), (rest, 0), (0, 0)))
+        + jnp.pad(from_west.astype(F32), ((0, 0), (0, rest), (0, 0)))
+        + jnp.pad(from_east.astype(F32), ((0, 0), (rest, 0), (0, 0)))
     )
     d_projected = jnp.concatenate([dq, owned.reshape(tokens, 2 * width).astype(BF16)], axis=1)
     grad_frame = (d_mid + nt(d_projected, weight_qkv)).astype(BF16)
 
-    both = ("lat", "lon")
-    devices = lat_n * lon_n
-    swap = [(i, i ^ 1) for i in range(devices)]
-    over_x, over_yz = chip_groups(lat_n, lon_n)
-    n_x, n_yz = len(over_x[0]), len(over_yz[0])
-    chips = n_x * n_yz
-
-    def exchange(blocks, groups):
-        return lax.all_to_all(blocks, both, 0, 0, axis_index_groups=groups)
-
-    other, other_gain = lax.ppermute((grads[1], gains[1]), both, swap)
-    held = (grads[0] + other).reshape(n_x, -1, 128)
-    held_gain = (gains[0] + other_gain).reshape(n_x, -1, 128)
-    n_main = held.shape[1]
-    held = jnp.sum(exchange(jnp.concatenate([held, held_gain], axis=1), over_x), axis=0)
-    held_gain = held[n_main:].reshape(n_yz, -1, 128)
-    held = held[:n_main].reshape(n_yz, -1, 128)
-    n_main = held.shape[1]
-    held = jnp.sum(exchange(jnp.concatenate([held, held_gain], axis=1), over_yz), axis=0) * grad_scale
-    body = held[:n_main].astype(BF16)
-    gain = held[n_main:]
-    high = gain.astype(BF16)
-    low = (gain - high.astype(F32)).astype(BF16)
-    mine = jnp.concatenate([body, high, low], axis=0)
-    n_rows = mine.shape[0]
-    mine = mine.reshape(1, -1, 2, 128)
-    mine = exchange(jnp.broadcast_to(mine, (n_yz,) + mine.shape[1:]), over_yz)
-    mine = mine.reshape((1,) + mine.shape)
-    mine = exchange(jnp.broadcast_to(mine, (n_x,) + mine.shape[1:]), over_x)
+    own = small_kernel(
+        functools.partial(finish_chunk, grad_scale), "finish_chunk", shape((n_yz, deep, 128), BF16), chunks
+    )
+    own = exchange(own, over_yz)
+    mine = small_kernel(join_chunks, "join_chunks", shape((n_x, 784, 128), BF16), own)
+    mine = exchange(mine, over_x)
     theirs = lax.ppermute(mine, both, swap)
-    first = jnp.where(core == 0, mine, theirs)
-    second = jnp.where(core == 0, theirs, mine)
-
-    def unpack(field):
-        flat_rows = field.reshape(chips, n_rows, 128)
-        blocks = flat_rows[:, :n_main].reshape(6, 2, 256, 128)
-        tail = flat_rows[:, n_main:, 0].astype(F32).reshape(chips, 2, -1)
-        return blocks, (tail[:, 0] + tail[:, 1]).reshape(-1)
-
-    first, sum_gain_attn = unpack(first)
-    second, sum_gain_mlp = unpack(second)
-
-    def beside(blocks):
-        return blocks.transpose(2, 0, 1, 3).reshape(256, -1)
-
+    gradients = small_kernel(
+        unpack,
+        "unpack",
+        [
+            shape((width, 3 * width), BF16),
+            shape((width, width), BF16),
+            shape((width, ff), BF16),
+            shape((ff, width), BF16),
+            shape((n_x, 128), F32),
+            shape((n_x, 128), F32),
+        ],
+        where,
+        mine,
+        theirs,
+    )
+    gain_sums = [g[:, : width // n_x].reshape(width) for g in gradients[4:]]
     return (
         block_out.reshape(rows, cols, width),
         grad_frame.reshape(rows, cols, width),
-        beside(jnp.concatenate([first[5:6], second[4:6]], axis=0)),
-        beside(first[4:5]),
-        beside(first[:4]),
-        second[:4].transpose(0, 2, 1, 3).reshape(ff, width),
-        sum_gain_attn,
-        sum_gain_mlp,
+        *gradients[:4],
+        *gain_sums,
     )
 
 

time: 183 us -> 184 us (level)
  blocking collectives: 75.6 us -> 36.8 us
  waiting for transfers between devices: 15.2 us -> 35.7 us
  starting transfers between devices: 48.5 us -> 65.1 us
  Pallas kernels: 20.7 us -> 30.2 us
  local copies, waits for them, and re-layouts: 12.7 us -> 8.09 us
    all_to_all x3 -> x2, blocking collectives: 75.6 us -> 36.8 us  [exchange(): return lax.all_to_all(blocks, both, 0, 0, axis_index_groups=groups)]
    all_to_all x1 -> x2, starting transfers between devices: 3.5 us -> 22.9 us  [exchange(): return lax.all_to_all(blocks, both, 0, 0, axis_index_groups=groups)]
    ppermute x6 -> x5, waiting for transfers between devices: 14.2 us -> 25 us  [the longest x1 18.8 us: on_device(): up = lax.ppermute(up, 'lat', north)]
    pallas_call x0 -> x4, Pallas kernels: none -> 9.16 us  [small_kernel(): pl.pallas_call(body, out_shape=outs, in_specs=[smem if a.dtype == jnp.int...]
    all_to_all x1 -> x2, waiting for transfers between devices: 0.01 us -> 8.89 us  [exchange(): return lax.all_to_all(blocks, both, 0, 0, axis_index_groups=groups)]
    reshape x3 -> x2, local copies, waits for them, and re-layouts: 0.4 us -> 2.62 us  [on_device(): gain_sums = [g[:, :width // n_x].reshape(width) for g in gradients[4:]]]
    slice x11 -> x1, local copies, waits for them, and re-layouts: 1.91 us -> 0.02 us  [on_device(): to_west = centre[:, cols + EDGE:].astype(BF16)]
    ppermute x6 -> x5, starting transfers between devices: 21.9 us -> 20.3 us  [the longest x1 7.8 us: on_device(): other = lax.ppermute(send, both, swap)]
  transfers between devices with their start and end apart: 12 -> 12, of which waited for: 6 -> 8; matrix products, arithmetic and copies ran while one was open for 3% -> 2% of each run, Pallas kernels for 0% -> 0%
where the time goes in v2:
time: 184 us; the launch traced here: 183 us
  starting transfers between devices  65.1 us (35%)
  blocking collectives  36.8 us (20%)
  waiting for transfers between devices  35.7 us (19%)
  Pallas kernels  30.2 us (16%)
  local copies, waits for them, and re-layouts  8.09 us (4%)
  other arithmetic  5.43 us (3%)
    all_to_all x2, blocking collectives, exchange(): return lax.all_to_all(blocks, both, 0, 0, axis_index_groups=groups)  36.8 us
    all_to_all x2, starting transfers between devices, exchange(): return lax.all_to_all(blocks, both, 0, 0, axis_index_groups=groups)  22.9 us
    pallas_call x1, Pallas kernels, local_part(): pl.pallas_call(functools.partial(local_kernel, dims), out_shape=outs, in_...  21 us
    ppermute x1, waiting for transfers between devices, on_device(): up = lax.ppermute(up, 'lat', north)  18.8 us
    pallas_call x4, Pallas kernels, small_kernel(): pl.pallas_call(body, out_shape=outs, in_specs=[smem if a.dtype == jnp.int...  9.16 us
    all_to_all x2, waiting for transfers between devices, exchange(): return lax.all_to_all(blocks, both, 0, 0, axis_index_groups=groups)  8.89 us
    ppermute x1, starting transfers between devices, on_device(): other = lax.ppermute(send, both, swap)  7.8 us
    ppermute x1, starting transfers between devices, on_device(): from_east = lax.ppermute(frame[:, :EDGE], 'lon', west)  6.17 us
  transfers between devices with their start and end apart: 12, of which 8 were waited for; matrix products, arithmetic and copies ran while one was open for 2% of the time, Pallas kernels for 0%

profile of v2, /device:TPU:1, one launch (start us, length us, event | category | flops | bytes accessed | tf_op | source)
XLA Modules:
  0.0 182.6 jit_solution(4863850739468829600)
XLA Ops:
  1.5 4.5 %collective-permute-start.1 = (bf16[16,8,256]{2,1,0:T(8,128)(2,1)S(1)}, bf16[16,8,256]{2,1,0:T(8,128)(2,1)S(1)}, u32[]{:S(2)}, u32[]{:S(2)}) collective-permute-start(bf16[16,8,256]{2,1,0:T(8,128)(2,1)S(1)} %get-tuple-element.54), channel_id=1, source_target_pairs={{0,1},{1,2},{2,3},{3,4},{4,5},{5,6},{6,7},{7,8},{8,9},{9,10},{10,1... | collective-permute-start | bytes 196616 | tf_op jit(solution)/shard_map/ppermute | solution.py:419
  6.0 6.2 %collective-permute-start = (bf16[16,8,256]{2,1,0:T(8,128)(2,1)S(1)}, bf16[16,8,256]{2,1,0:T(8,128)(2,1)S(1)}, u32[]{:S(2)}, u32[]{:S(2)}) collective-permute-start(bf16[16,8,256]{2,1,0:T(8,128)(2,1)S(1)} %get-tuple-element.55), channel_id=1, source_target_pairs={{1,0},{2,1},{3,2},{4,3},{5,4},{6,5},{7,6},{8,7},{9,8},{10,9},{11,1... | collective-permute-start | bytes 196616 | tf_op jit(solution)/shard_map/ppermute | solution.py:418
  14.5 5.5 %collective-permute-start.2 = (bf16[6,32,256]{2,1,0:T(8,128)(2,1)S(1)}, bf16[6,32,256]{2,1,0:T(8,128)(2,1)S(1)}, u32[]{:S(2)}, u32[]{:S(2)}) collective-permute-start(bf16[6,32,256]{2,1,0:T(8,128)(2,1)S(1)} %get-tuple-element.53), channel_id=1, source_target_pairs={{0,32},{32,64},{64,96},{96,128},{128,160},{160,192},{192,224},{224... | collective-permute-start | bytes 294920 | tf_op jit(solution)/shard_map/ppermute | solution.py:422
  22.3 21.0 %local_part.1 = (bf16[256,256]{1,0:T(8,128)(2,1)}, f32[256,256]{1,0:T(8,128)}, bf16[256,256]{1,0:T(8,128)(2,1)}, bf16[192,512]{1,0:T(8,128)(2,1)}, bf16[192,512]...) custom-call(s32[2]{0:T(128)} %pad_add_fusion.where_ref, ...), custom_call_target="tpu_custom_call" | custom-call | tf_op jit(solution)/shard_map/local_part/pallas_call | solution.py:266
  43.3 7.8 %collective-permute-start.4 = (f32[3328,128]{1,0:T(8,128)}, f32[3328,128]{1,0:T(8,128)S(1)}, u32[]{:S(2)}, u32[]{:S(2)}) collective-permute-start(f32[3328,128]{1,0:T(8,128)} %get-tuple-element.33), channel_id=1, source_target_pairs={{0,1},{1,0},{2,3},{3,2},{4,5},{5,4},{6,7},{7,6},{8,9},{9,8},{10,11... | collective-permute-start | bytes 5111816 | tf_op jit(solution)/shard_map/ppermute | solution.py:457
  51.1 3.4 %collective-permute-done.4 = f32[3328,128]{1,0:T(8,128)S(1)} collective-permute-done((f32[3328,128]{1,0:T(8,128)}, f32[3328,128]{1,0:T(8,128)S(1)}, u32[]{:S(2)}, u32[]{:S(2)}) %collective-permute-start.4) | collective-permute-done | bytes 1703968 | tf_op jit(solution)/shard_map/ppermute | solution.py:457
  55.5 1.6 slice_add_fusion
  57.1 1.3 pad_maximum_fusion
  58.4 5.0 %all-to-all-start = ((f32[4,832,128]{2,1,0:T(8,128)}), f32[4,832,128]{2,1,0:T(8,128)S(1)}, u32[]{:S(2)}, u32[]{:S(2)}) async-start(f32[4,832,128]{2,1,0:T(8,128)} %pad_maximum_fusion), calls=%async_computation | async-start | bytes 3407872 | tf_op jit(solution)/shard_map/all_to_all | solution.py:452
  63.4 1.4 collective-permute-start.5
  64.9 5.5 %collective-permute-start.6 = (bf16[192,512]{1,0:T(8,128)(2,1)S(1)}, bf16[192,512]{1,0:T(8,128)(2,1)S(1)}, u32[]{:S(2)}, u32[]{:S(2)}) collective-permute-start(bf16[192,512]{1,0:T(8,128)(2,1)S(1)} %copy-done.10), channel_id=1, source_target_pairs={{0,32},{32,64},{64,96},{96,128},{128,160},{160,192},{192,224},{224... | collective-permute-start | bytes 589832 | tf_op jit(solution)/shard_map/ppermute | solution.py:455
  70.4 18.8 %collective-permute-done.5 = bf16[192,512]{1,0:T(8,128)(2,1)S(1)} collective-permute-done((bf16[192,512]{1,0:T(8,128)(2,1)S(1)}, bf16[192,512]{1,0:T(8,128)(2,1)S(1)}, u32[]{:S(2)}, u32[]{:S(2)}) %collective-permute-start.5) | collective-permute-done | bytes 196640 | tf_op jit(solution)/shard_map/ppermute | solution.py:454
  91.3 2.3 %pack_chunks.1 = f32[64,16,128]{2,1,0:T(8,128)} custom-call(f32[4,832,128]{2,1,0:T(8,128)} %copy-done), custom_call_target="tpu_custom_call" | custom-call | tf_op jit(solution)/shard_map/pack_chunks/pallas_call | solution.py:297
  93.6 17.8 %all-to-all-start.1 = ((f32[64,16,128]{2,1,0:T(8,128)}), f32[64,16,128]{2,1,0:T(8,128)S(1)}, u32[]{:S(2)}, u32[]{:S(2)}) async-start(f32[64,16,128]{2,1,0:T(8,128)} %pack_chunks.1), calls=%async_computation.1 | async-start | bytes 1048576 | tf_op jit(solution)/shard_map/all_to_all | solution.py:452
  111.7 3.4 %collective-permute-start.8 = (bf16[16,8,512]{2,1,0:T(8,128)(2,1)S(1)}, bf16[16,8,512]{2,1,0:T(8,128)(2,1)S(1)}, u32[]{:S(2)}, u32[]{:S(2)}) collective-permute-start(bf16[16,8,512]{2,1,0:T(8,128)(2,1)S(1)} %get-tuple-element.50), channel_id=1, source_target_pairs={{1,0},{2,1},{3,2},{4,3},{5,4},{6,5},{7,6},{8,7},{9,8},{10,9},{11,1... | collective-permute-start | bytes 393224 | tf_op jit(solution)/shard_map/ppermute | solution.py:471
  115.2 2.1 %collective-permute-start.7 = (bf16[16,8,512]{2,1,0:T(8,128)(2,1)S(1)}, bf16[16,8,512]{2,1,0:T(8,128)(2,1)S(1)}, u32[]{:S(2)}, u32[]{:S(2)}) collective-permute-start(bf16[16,8,512]{2,1,0:T(8,128)(2,1)S(1)} %get-tuple-element.51), channel_id=1, source_target_pairs={{0,1},{1,2},{2,3},{3,4},{4,5},{5,6},{6,7},{7,8},{8,9},{9,10},{10,1... | collective-permute-start | bytes 393224 | tf_op jit(solution)/shard_map/ppermute | solution.py:470
  119.3 8.9 %all-to-all-done.1.chunks_ref = f32[64,16,128]{2,1,0:T(8,128)S(1)} async-done(((f32[64,16,128]{2,1,0:T(8,128)}), f32[64,16,128]{2,1,0:T(8,128)S(1)}, u32[]{:S(2)}, u32[]{:S(2)}) %all-to-all-start.1) | async-done | bytes 524320 | tf_op jit(solution)/shard_map/all_to_all | solution.py:452
  128.9 1.8 %finish_chunk.1 = bf16[64,16,128]{2,1,0:T(8,128)(2,1)} custom-call(f32[64,16,128]{2,1,0:T(8,128)} %copy-done.2), custom_call_target="tpu_custom_call" | custom-call | tf_op jit(solution)/shard_map/finish_chunk/pallas_call | solution.py:297
  130.8 19.7 %all_to_all.20.chunks_ref = bf16[64,16,128]{2,1,0:T(8,128)(2,1)} all-to-all(bf16[64,16,128]{2,1,0:T(8,128)(2,1)} %finish_chunk.1), channel_id=1, replica_groups={{0,4,8,12,16,20,24,28,64,68,72,76,80,84,88,92,128,132,136,140,144,148,1..., dimensions={0} | all-to-all | bytes 524288 | tf_op jit(solution)/shard_map/all_to_all | solution.py:452
  150.5 2.1 %join_chunks.1 = bf16[4,784,128]{2,1,0:T(8,128)(2,1)} custom-call(bf16[64,16,128]{2,1,0:T(8,128)(2,1)} %all_to_all.20.chunks_ref), custom_call_target="tpu_custom_call" | custom-call | tf_op jit(solution)/shard_map/join_chunks/pallas_call | solution.py:297
  152.6 17.1 %all_to_all.21.mine_ref = bf16[4,784,128]{2,1,0:T(8,128)(2,1)S(1)} all-to-all(bf16[4,784,128]{2,1,0:T(8,128)(2,1)} %join_chunks.1), channel_id=1, replica_groups={{0,2,32,34},{1,3,33,35},{4,6,36,38},{5,7,37,39},{8,10,40,42},{9,11,41,4..., dimensions={0} | all-to-all | bytes 1605632 | tf_op jit(solution)/shard_map/all_to_all | solution.py:452
  169.7 4.5 %collective-permute-start.9 = (bf16[4,784,128]{2,1,0:T(8,128)(2,1)S(1)}, bf16[4,784,128]{2,1,0:T(8,128)(2,1)S(1)}, u32[]{:S(2)}, u32[]{:S(2)}) collective-permute-start(bf16[4,784,128]{2,1,0:T(8,128)(2,1)S(1)} %all_to_all.21.mine_ref), channel_id=1, source_target_pairs={{0,1},{1,0},{2,3},{3,2},{4,5},{5,4},{6,7},{7,6},{8,9},{9,8},{10,11... | collective-permute-start | bytes 2408456 | tf_op jit(solution)/shard_map/ppermute | solution.py:495
  177.1 2.9 %unpack.1 = (bf16[256,768]{1,0:T(8,128)(2,1)}, bf16[256,256]{1,0:T(8,128)(2,1)}, bf16[256,1024]{1,0:T(8,128)(2,1)}, bf16[1024,256]{1,0:T(8,128)(2,1)}, f32[4,128]{1,0:T(4,128)}, /*index=5*/f32[4,128]{1,0:T(4,128)}) custom-call(s32[2]{0:T(128)} %pad_add_fusion.where_ref, bf16[4,784,128]{2,1,0:T(8,128)(2,1)} %copy-done.1, bf16[4,784,128]{2,1,0:T(8,128)(2,1)} %copy-done.5), custom_call_target="tpu_custom_call" | custom-call | tf_op jit(solution)/shard_map/unpack/pallas_call | solution.py:297
  179.9 1.3 reshape.78
  (49 shorter events, 15.5 us)
Async XLA Ops:
  1.5 11.6 %collective-permute-start.1 = (bf16[16,8,256]{2,1,0:T(8,128)(2,1)S(1)}, bf16[16,8,256]{2,1,0:T(8,128)(2,1)S(1)}, u32[]{:S(2)}, u32[]{:S(2)}) collective-permute-start(bf16[16,8,256]{2,1,0:T(8,128)(2,1)S(1)} %get-tuple-element.54), channel_id=1, source_target_pairs={{0,1},{1,2},{2,3},{3,4},{4,5},{5,6},{6,7},{7,8},{8,9},{9,10},{10,1... | collective-permute-start | bytes 196616 | tf_op jit(solution)/shard_map/ppermute | solution.py:419
  6.0 7.1 %collective-permute-start = (bf16[16,8,256]{2,1,0:T(8,128)(2,1)S(1)}, bf16[16,8,256]{2,1,0:T(8,128)(2,1)S(1)}, u32[]{:S(2)}, u32[]{:S(2)}) collective-permute-start(bf16[16,8,256]{2,1,0:T(8,128)(2,1)S(1)} %get-tuple-element.55), channel_id=1, source_target_pairs={{1,0},{2,1},{3,2},{4,3},{5,4},{6,5},{7,6},{8,7},{9,8},{10,9},{11,1... | collective-permute-start | bytes 196616 | tf_op jit(solution)/shard_map/ppermute | solution.py:418
  13.2 8.5 %copy-start.3 = (bf16[16,32,256]{2,1,0:T(8,128)(2,1)}, bf16[16,32,256]{2,1,0:T(8,128)(2,1)S(1)}, u32[]{:S(2)}) copy-start(bf16[16,32,256]{2,1,0:T(8,128)(2,1)S(1)} %constant_dynamic-update-slice_fusion) | copy-start | bytes 786436
  13.2 7.4 %collective-permute-start.3 = (bf16[6,32,256]{2,1,0:T(8,128)(2,1)S(1)}, bf16[6,32,256]{2,1,0:T(8,128)(2,1)S(1)}, u32[]{:S(2)}, u32[]{:S(2)}) collective-permute-start(bf16[6,32,256]{2,1,0:T(8,128)(2,1)S(1)} %get-tuple-element.52), channel_id=1, source_target_pairs={{32,0},{64,32},{96,64},{128,96},{160,128},{192,160},{224,192},{256... | collective-permute-start | bytes 294920 | tf_op jit(solution)/shard_map/ppermute | solution.py:421
  14.5 7.1 %collective-permute-start.2 = (bf16[6,32,256]{2,1,0:T(8,128)(2,1)S(1)}, bf16[6,32,256]{2,1,0:T(8,128)(2,1)S(1)}, u32[]{:S(2)}, u32[]{:S(2)}) collective-permute-start(bf16[6,32,256]{2,1,0:T(8,128)(2,1)S(1)} %get-tuple-element.53), channel_id=1, source_target_pairs={{0,32},{32,64},{64,96},{96,128},{128,160},{160,192},{192,224},{224... | collective-permute-start | bytes 294920 | tf_op jit(solution)/shard_map/ppermute | solution.py:422
  20.6 1.0 copy-start.8
  43.3 11.2 %collective-permute-start.4 = (f32[3328,128]{1,0:T(8,128)}, f32[3328,128]{1,0:T(8,128)S(1)}, u32[]{:S(2)}, u32[]{:S(2)}) collective-permute-start(f32[3328,128]{1,0:T(8,128)} %get-tuple-element.33), channel_id=1, source_target_pairs={{0,1},{1,0},{2,3},{3,2},{4,5},{5,4},{6,7},{7,6},{8,9},{9,8},{10,11... | collective-permute-start | bytes 5111816 | tf_op jit(solution)/shard_map/ppermute | solution.py:457
  58.4 5.0 %copy-start.11 = (bf16[192,512]{1,0:T(8,128)(2,1)S(1)}, bf16[192,512]{1,0:T(8,128)(2,1)}, u32[]{:S(2)}) copy-start(bf16[192,512]{1,0:T(8,128)(2,1)} %get-tuple-element.34) | copy-start | bytes 589828
  58.4 6.5 %copy-start.10 = (bf16[192,512]{1,0:T(8,128)(2,1)S(1)}, bf16[192,512]{1,0:T(8,128)(2,1)}, u32[]{:S(2)}) copy-start(bf16[192,512]{1,0:T(8,128)(2,1)} %get-tuple-element.35) | copy-start | bytes 589828
  58.4 31.6 %all-to-all-start = ((f32[4,832,128]{2,1,0:T(8,128)}), f32[4,832,128]{2,1,0:T(8,128)S(1)}, u32[]{:S(2)}, u32[]{:S(2)}) async-start(f32[4,832,128]{2,1,0:T(8,128)} %pad_maximum_fusion), calls=%async_computation | async-start | bytes 3407872 | tf_op jit(solution)/shard_map/all_to_all | solution.py:452
  63.4 48.0 %copy-start.4 = (f32[512,512]{1,0:T(8,128)S(1)}, f32[512,512]{1,0:T(8,128)}, u32[]{:S(2)}) copy-start(f32[512,512]{1,0:T(8,128)} %get-tuple-element.31) | copy-start | bytes 3145732
  63.4 25.8 %collective-permute-start.5 = (bf16[192,512]{1,0:T(8,128)(2,1)S(1)}, bf16[192,512]{1,0:T(8,128)(2,1)S(1)}, u32[]{:S(2)}, u32[]{:S(2)}) collective-permute-start(bf16[192,512]{1,0:T(8,128)(2,1)S(1)} %copy-done.11), channel_id=1, source_target_pairs={{32,0},{64,32},{96,64},{128,96},{160,128},{192,160},{224,192},{256... | collective-permute-start | bytes 589832 | tf_op jit(solution)/shard_map/ppermute | solution.py:454
  64.9 25.2 %collective-permute-start.6 = (bf16[192,512]{1,0:T(8,128)(2,1)S(1)}, bf16[192,512]{1,0:T(8,128)(2,1)S(1)}, u32[]{:S(2)}, u32[]{:S(2)}) collective-permute-start(bf16[192,512]{1,0:T(8,128)(2,1)S(1)} %copy-done.10), channel_id=1, source_target_pairs={{0,32},{32,64},{64,96},{96,128},{128,160},{160,192},{192,224},{224... | collective-permute-start | bytes 589832 | tf_op jit(solution)/shard_map/ppermute | solution.py:455
  90.1 1.2 copy-start
  93.6 34.5 %all-to-all-start.1 = ((f32[64,16,128]{2,1,0:T(8,128)}), f32[64,16,128]{2,1,0:T(8,128)S(1)}, u32[]{:S(2)}, u32[]{:S(2)}) async-start(f32[64,16,128]{2,1,0:T(8,128)} %pack_chunks.1), calls=%async_computation.1 | async-start | bytes 1048576 | tf_op jit(solution)/shard_map/all_to_all | solution.py:452
  111.7 6.6 %collective-permute-start.8 = (bf16[16,8,512]{2,1,0:T(8,128)(2,1)S(1)}, bf16[16,8,512]{2,1,0:T(8,128)(2,1)S(1)}, u32[]{:S(2)}, u32[]{:S(2)}) collective-permute-start(bf16[16,8,512]{2,1,0:T(8,128)(2,1)S(1)} %get-tuple-element.50), channel_id=1, source_target_pairs={{1,0},{2,1},{3,2},{4,3},{5,4},{6,5},{7,6},{8,7},{9,8},{10,9},{11,1... | collective-permute-start | bytes 393224 | tf_op jit(solution)/shard_map/ppermute | solution.py:471
  115.2 4.1 %collective-permute-start.7 = (bf16[16,8,512]{2,1,0:T(8,128)(2,1)S(1)}, bf16[16,8,512]{2,1,0:T(8,128)(2,1)S(1)}, u32[]{:S(2)}, u32[]{:S(2)}) collective-permute-start(bf16[16,8,512]{2,1,0:T(8,128)(2,1)S(1)} %get-tuple-element.51), channel_id=1, source_target_pairs={{0,1},{1,2},{2,3},{3,4},{4,5},{5,6},{6,7},{7,8},{8,9},{9,10},{10,1... | collective-permute-start | bytes 393224 | tf_op jit(solution)/shard_map/ppermute | solution.py:470
  128.1 0.8 copy-start.2
  150.5 23.8 %copy-start.6 = (bf16[256,768]{1,0:T(8,128)(2,1)S(1)}, bf16[256,768]{1,0:T(8,128)(2,1)}, u32[]{:S(2)}) copy-start(bf16[256,768]{1,0:T(8,128)(2,1)} %wqkv_ref.1) | copy-start | bytes 1179652
  150.5 23.8 %copy-start.12 = (bf16[256,256]{1,0:T(8,128)(2,1)S(1)}, bf16[256,256]{1,0:T(8,128)(2,1)}, u32[]{:S(2)}) copy-start(bf16[256,256]{1,0:T(8,128)(2,1)} %get-tuple-element.30) | copy-start | bytes 393220
  152.6 22.0 %copy-start.7 = (f32[256,256]{1,0:T(8,128)S(1)}, f32[256,256]{1,0:T(8,128)}, u32[]{:S(2)}) copy-start(f32[256,256]{1,0:T(8,128)} %get-tuple-element.29) | copy-start | bytes 786436
  169.7 6.4 %copy-start.1 = (bf16[4,784,128]{2,1,0:T(8,128)(2,1)}, bf16[4,784,128]{2,1,0:T(8,128)(2,1)S(1)}, u32[]{:S(2)}) copy-start(bf16[4,784,128]{2,1,0:T(8,128)(2,1)S(1)} %all_to_all.21.mine_ref) | copy-start | bytes 2408452
  169.7 6.4 %collective-permute-start.9 = (bf16[4,784,128]{2,1,0:T(8,128)(2,1)S(1)}, bf16[4,784,128]{2,1,0:T(8,128)(2,1)S(1)}, u32[]{:S(2)}, u32[]{:S(2)}) collective-permute-start(bf16[4,784,128]{2,1,0:T(8,128)(2,1)S(1)} %all_to_all.21.mine_ref), channel_id=1, source_target_pairs={{0,1},{1,0},{2,3},{3,2},{4,5},{5,4},{6,7},{7,6},{8,9},{9,8},{10,11... | collective-permute-start | bytes 2408456 | tf_op jit(solution)/shard_map/ppermute | solution.py:495
  176.1 0.9 copy-start.5
  (1 other events, 0.6 us)

commit v3 on v2

--- a/solution.py
+++ b/solution.py
@@ -18,6 +18,7 @@
 
 F32 = jnp.float32
 BF16 = jnp.bfloat16
+TOP = 14.0
 
 
 def nn(left, right):
@@ -307,29 +308,51 @@
     return lax.broadcasted_iota(jnp.int32, shape, 1)
 
 
-def pack_chunks(n, parts_ref, chunks_ref):
-    total = parts_ref[0]
-    for k in range(1, parts_ref.shape[0]):
-        total = total + parts_ref[k]
-    deep = 512 // n
-    chunks_ref[:, :deep] = total[:512].reshape(n, deep, 128)
+def pack_chunks(keep_ref, other_ref, chunks_ref):
+    n = chunks_ref.shape[0] // 4
     half = n // 2
-    tail = total[512:768].reshape(half, deep, 128)
-    gain = total[768:].reshape(n, -1, 128)[:, :1]
-    row = first_rows(tail.shape)
-    for i in range(2):
-        piece = tail if i == 0 else pltpu.roll(tail, deep // 2, 1)
-        mine = gain[i * half : (i + 1) * half]
-        chunks_ref[i * half : (i + 1) * half, deep:] = jnp.where(row < deep // 2, piece, mine)
+
+    def scaled(value):
+        largest = jnp.maximum(jnp.max(jnp.abs(value), axis=(0, 1), keepdims=True), 1e-37)
+        power = jnp.clip(jnp.ceil(jnp.log2(largest)), -100.0, 127.0)
+        return value * jnp.exp2(TOP - power), power
+
+    gain, gain_power = scaled(keep_ref[3072:, :] + other_ref[3072:, :])
+    gain = gain.reshape(4, n, 1, 128)
+    row = lax.broadcasted_iota(jnp.int32, (half, 8, 128), 1)
+    for k in range(4):
+        first = k * 768
+        powers = []
+        for i in range(2):
+            at = first + i * 256
+            value, power = scaled(keep_ref[at : at + 256, :] + other_ref[at : at + 256, :])
+            powers.append(power)
+            chunks_ref[k * n + i * half : k * n + (i + 1) * half, :8] = value.reshape(half, 8, 128)
+        at = first + 512
+        tail, tail_power = scaled(keep_ref[at : at + 256, :] + other_ref[at : at + 256, :])
+        tail = tail.reshape(half, 8, 128)
+        for i in range(2):
+            piece = tail if i == 0 else pltpu.roll(tail, 4, 1)
+            piece = jnp.where(row < 4, piece, gain[k, i * half : (i + 1) * half])
+            for at_row, power in ((5, powers[i]), (6, tail_power), (7, gain_power)):
+                piece = jnp.where(row == at_row, power.reshape(1, 1, 1), piece)
+            chunks_ref[k * n + i * half : k * n + (i + 1) * half, 8:] = piece
 
 
 def finish_chunk(scale, chunks_ref, own_ref):
-    n, deep = chunks_ref.shape[0], chunks_ref.shape[1] // 2
-    total = jnp.sum(chunks_ref[...], axis=0) * scale
-    high = total.astype(BF16).astype(F32)
-    row = lax.broadcasted_iota(jnp.int32, total.shape, 0)
-    total = jnp.where(row == total.shape[0] - 1, total - high, total).astype(BF16)
-    own_ref[...] = jnp.broadcast_to(total[None], (n,) + total.shape)
+    body = chunks_ref[:, :8]
+    tail = chunks_ref[:, 8:]
+    factor = jnp.exp2(tail - TOP)
+    body = jnp.sum(body * factor[:, 5:6], axis=0)
+    row = lax.broadcasted_iota(jnp.int32, tail.shape, 1)
+    factor = jnp.where(row < 4, factor[:, 6:7], factor[:, 7:8])
+    tail = jnp.sum(jnp.where(row < 5, tail * factor, 0.0), axis=0) * scale
+    gain = tail[4:5]
+    high = gain.astype(BF16).astype(F32)
+    row = lax.broadcasted_iota(jnp.int32, tail.shape, 0)
+    tail = jnp.where(row == 6, high, jnp.where(row == 7, gain - high, tail))
+    total = jnp.concatenate([body * scale, tail], axis=0).astype(BF16)
+    own_ref[...] = jnp.broadcast_to(total[None], own_ref.shape)
 
 
 def join_chunks(chunks_ref, rows_ref):
@@ -368,9 +391,11 @@
                 target, column = qkv_ref, 0
             lane = column * 256 + right * 128
             target[:, lane : lane + 128] = value
-        for k in range(rows_ref.shape[0]):
-            gain = rows_ref[k, 768:, :].astype(F32)
-            gain_ref[k : k + 1, :] = (gain + pltpu.roll(gain, 64, 1))[:1]
+        lane = lax.broadcasted_iota(jnp.int32, (16, 128), 1)
+        for k in range(0, rows_ref.shape[0], 2):
+            gain = [rows_ref[k + i, 768:, :].astype(F32) for i in range(2)]
+            gain = [g + pltpu.roll(g, 64, 1) for g in gain]
+            gain_ref[:, k * 64 : k * 64 + 128] = jnp.where(lane < 64, *gain)[:1]
 
     @pl.when(where_ref[1] == 0)
     def _():
@@ -394,7 +419,10 @@
     over_yz = [
         [flat(z, x, y, core) for z in range(n_z) for y in range(n_y)] for x in range(4) for core in range(2)
     ]
-    return over_x, over_yz
+    over_chips = [
+        [flat(z, x, y, core) for x in range(4) for z in range(n_z) for y in range(n_y)] for core in range(2)
+    ]
+    return over_x, over_yz, over_chips
 
 
 def on_device(
@@ -444,7 +472,7 @@
     both = ("lat", "lon")
     devices = lat_n * lon_n
     swap = [(i, i ^ 1) for i in range(devices)]
-    over_x, over_yz = chip_groups(lat_n, lon_n)
+    over_x, over_yz, over_chips = chip_groups(lat_n, lon_n)
     n_x, n_yz = len(over_x[0]), len(over_yz[0])
     shape = jax.ShapeDtypeStruct
 
@@ -455,10 +483,9 @@
     down = lax.ppermute(down, "lat", south)
 
     other = lax.ppermute(send, both, swap)
-    pieces = (keep[:3072] + other[:3072]).reshape(n_x, 768, 128)
-    tails = (keep[3072:] + other[3072:]).reshape(n_x, -1, 128)
-    parts = exchange(jnp.concatenate([pieces, tails], axis=1), over_x)
-    parts, up, down = lax.optimization_barrier((parts, up, down))
+    chunks = small_kernel(pack_chunks, "pack_chunks", shape((n_x * n_yz, 16, 128), F32), keep, other)
+    chunks = exchange(chunks.astype(jnp.float16), over_chips)
+    chunks, up, down = lax.optimization_barrier((chunks, up, down))
 
     up = up.reshape(RADIUS, across, 2 * width).astype(F32)
     down = down.reshape(RADIUS, across, 2 * width).astype(F32)
@@ -470,12 +497,14 @@
     from_west = lax.ppermute(to_east, "lon", east)
     from_east = lax.ppermute(to_west, "lon", west)
 
-    deep = 2 * 512 // n_yz
-    chunks = small_kernel(
-        functools.partial(pack_chunks, n_yz), "pack_chunks", shape((n_yz, deep, 128), F32), parts
-    )
-    chunks = exchange(chunks, over_yz)
-    chunks, from_west, from_east = lax.optimization_barrier((chunks, from_west, from_east))
+    own = small_kernel(
+        functools.partial(finish_chunk, grad_scale),
+        "finish_chunk",
+        shape((n_yz, 16, 128), BF16),
+        chunks.astype(F32),
+    )
+    own = exchange(own, over_yz)
+    own, from_west, from_east = lax.optimization_barrier((own, from_west, from_east))
 
     rest = cols - EDGE
     owned = (
@@ -486,10 +515,6 @@
     d_projected = jnp.concatenate([dq, owned.reshape(tokens, 2 * width).astype(BF16)], axis=1)
     grad_frame = (d_mid + nt(d_projected, weight_qkv)).astype(BF16)
 
-    own = small_kernel(
-        functools.partial(finish_chunk, grad_scale), "finish_chunk", shape((n_yz, deep, 128), BF16), chunks
-    )
-    own = exchange(own, over_yz)
     mine = small_kernel(join_chunks, "join_chunks", shape((n_x, 784, 128), BF16), own)
     mine = exchange(mine, over_x)
     theirs = lax.ppermute(mine, both, swap)
@@ -501,14 +526,14 @@
             shape((width, width), BF16),
             shape((width, ff), BF16),
             shape((ff, width), BF16),
-            shape((n_x, 128), F32),
-            shape((n_x, 128), F32),
+            shape((1, width), F32),
+            shape((1, width), F32),
         ],
         where,
         mine,
         theirs,
     )
-    gain_sums = [g[:, : width // n_x].reshape(width) for g in gradients[4:]]
+    gain_sums = [g.reshape(width) for g in gradients[4:]]
     return (
         block_out.reshape(rows, cols, width),
         grad_frame.reshape(rows, cols, width),

time: 184 us -> 168 us (0.913)
  blocking collectives: 36.8 us -> 12.9 us
  starting transfers between devices: 65.1 us -> 73.5 us
  local copies, waits for them, and re-layouts: 8.09 us -> 5.38 us
  Pallas kernels: 30.2 us -> 32.8 us
    all_to_all x2 -> x1, blocking collectives: 36.8 us -> 12.9 us  [exchange(): return lax.all_to_all(blocks, both, 0, 0, axis_index_groups=groups)]
    ppermute x1, waiting for transfers between devices: 18.8 us -> 5.26 us  [on_device(): up = lax.ppermute(up, 'lat', north)]
    all_to_all x2, waiting for transfers between devices: 8.89 us -> 18.3 us  [exchange(): return lax.all_to_all(blocks, both, 0, 0, axis_index_groups=groups)]
    all_to_all x2, starting transfers between devices: 22.9 us -> 29.5 us  [exchange(): return lax.all_to_all(blocks, both, 0, 0, axis_index_groups=groups)]
    convert_element_type x0 -> x2, other arithmetic: none -> 4.24 us  [the longest x1 2.72 us: on_device(): chunks = exchange(chunks.astype(jnp.float16), over_chips)]
    reshape x2 -> x0, local copies, waits for them, and re-layouts: 2.62 us -> none  [on_device(): gain_sums = [g[:, :width // n_x].reshape(width) for g in gradients[4:]]]
    add x2 -> x0, other arithmetic: 2.54 us -> none  [the longest x1 1.61 us: on_device(): pieces = (keep[:3072] + other[:3072]).reshape(n_x, 768, 128)]
    pallas_call x4, Pallas kernels: 9.16 us -> 11.7 us  [small_kernel(): pl.pallas_call(body, out_shape=outs, in_specs=[smem if a.dtype == jnp.int...]
  transfers between devices with their start and end apart: 12 -> 12, of which waited for: 8 -> 9; matrix products, arithmetic and copies ran while one was open for 2% -> 2% of each run, Pallas kernels for 0% -> 0%
where the time goes in v3:
time: 168 us; the launch traced here: 167 us
  starting transfers between devices  73.5 us (44%)
  waiting for transfers between devices  35.1 us (21%)
  Pallas kernels  32.8 us (20%)
  blocking collectives  12.9 us (8%)
  other arithmetic  5.88 us (4%)
  local copies, waits for them, and re-layouts  5.38 us (3%)
    all_to_all x2, starting transfers between devices, exchange(): return lax.all_to_all(blocks, both, 0, 0, axis_index_groups=groups)  29.5 us
    pallas_call x1, Pallas kernels, local_part(): pl.pallas_call(functools.partial(local_kernel, dims), out_shape=outs, in_...  21.1 us
    all_to_all x2, waiting for transfers between devices, exchange(): return lax.all_to_all(blocks, both, 0, 0, axis_index_groups=groups)  18.3 us
    all_to_all x1, blocking collectives, exchange(): return lax.all_to_all(blocks, both, 0, 0, axis_index_groups=groups)  12.9 us
    pallas_call x4, Pallas kernels, small_kernel(): pl.pallas_call(body, out_shape=outs, in_specs=[smem if a.dtype == jnp.int...  11.7 us
    ppermute x1, starting transfers between devices, on_device(): other = lax.ppermute(send, both, swap)  7.8 us
    ppermute x1, starting transfers between devices, on_device(): from_east = lax.ppermute(frame[:, :EDGE], 'lon', west)  6.17 us
    ppermute x1, starting transfers between devices, on_device(): theirs = lax.ppermute(mine, both, swap)  6.03 us
  transfers between devices with their start and end apart: 12, of which 9 were waited for; matrix products, arithmetic and copies ran while one was open for 2% of the time, Pallas kernels for 0%

profile of v3, /device:TPU:1, one launch (start us, length us, event | category | flops | bytes accessed | tf_op | source)
XLA Modules:
  0.0 166.7 jit_solution(10110738032207537666)
XLA Ops:
  1.5 4.5 %collective-permute-start.1 = (bf16[16,8,256]{2,1,0:T(8,128)(2,1)S(1)}, bf16[16,8,256]{2,1,0:T(8,128)(2,1)S(1)}, u32[]{:S(2)}, u32[]{:S(2)}) collective-permute-start(bf16[16,8,256]{2,1,0:T(8,128)(2,1)S(1)} %get-tuple-element.54), channel_id=1, source_target_pairs={{0,1},{1,2},{2,3},{3,4},{4,5},{5,6},{6,7},{7,8},{8,9},{9,10},{10,1... | collective-permute-start | bytes 196616 | tf_op jit(solution)/shard_map/ppermute | solution.py:447
  6.0 6.2 %collective-permute-start = (bf16[16,8,256]{2,1,0:T(8,128)(2,1)S(1)}, bf16[16,8,256]{2,1,0:T(8,128)(2,1)S(1)}, u32[]{:S(2)}, u32[]{:S(2)}) collective-permute-start(bf16[16,8,256]{2,1,0:T(8,128)(2,1)S(1)} %get-tuple-element.55), channel_id=1, source_target_pairs={{1,0},{2,1},{3,2},{4,3},{5,4},{6,5},{7,6},{8,7},{9,8},{10,9},{11,1... | collective-permute-start | bytes 196616 | tf_op jit(solution)/shard_map/ppermute | solution.py:446
  14.5 5.5 %collective-permute-start.2 = (bf16[6,32,256]{2,1,0:T(8,128)(2,1)S(1)}, bf16[6,32,256]{2,1,0:T(8,128)(2,1)S(1)}, u32[]{:S(2)}, u32[]{:S(2)}) collective-permute-start(bf16[6,32,256]{2,1,0:T(8,128)(2,1)S(1)} %get-tuple-element.53), channel_id=1, source_target_pairs={{0,32},{32,64},{64,96},{96,128},{128,160},{160,192},{192,224},{224... | collective-permute-start | bytes 294920 | tf_op jit(solution)/shard_map/ppermute | solution.py:450
  22.3 21.1 %local_part.1 = (bf16[256,256]{1,0:T(8,128)(2,1)}, f32[256,256]{1,0:T(8,128)}, bf16[256,256]{1,0:T(8,128)(2,1)}, bf16[192,512]{1,0:T(8,128)(2,1)}, bf16[192,512]...) custom-call(s32[2]{0:T(128)} %pad_add_fusion.where_ref, ...), custom_call_target="tpu_custom_call" | custom-call | tf_op jit(solution)/shard_map/local_part/pallas_call | solution.py:267
  43.3 7.8 %collective-permute-start.4 = (f32[3328,128]{1,0:T(8,128)}, f32[3328,128]{1,0:T(8,128)S(1)}, u32[]{:S(2)}, u32[]{:S(2)}) collective-permute-start(f32[3328,128]{1,0:T(8,128)} %get-tuple-element.33), channel_id=1, source_target_pairs={{0,1},{1,0},{2,3},{3,2},{4,5},{5,4},{6,7},{7,6},{8,9},{9,8},{10,11... | collective-permute-start | bytes 5111816 | tf_op jit(solution)/shard_map/ppermute | solution.py:485
  51.2 3.4 %collective-permute-done.4.other_ref = f32[3328,128]{1,0:T(8,128)S(1)} collective-permute-done((f32[3328,128]{1,0:T(8,128)}, f32[3328,128]{1,0:T(8,128)S(1)}, u32[]{:S(2)}, u32[]{:S(2)}) %collective-permute-start.4) | collective-permute-done | bytes 1703968 | tf_op jit(solution)/shard_map/ppermute | solution.py:485
  55.8 3.9 %pack_chunks.1 = f32[256,16,128]{2,1,0:T(8,128)} custom-call(f32[3328,128]{1,0:T(8,128)} %get-tuple-element.32.keep_ref, f32[3328,128]{1,0:T(8,128)} %copy-done.1), custom_call_target="tpu_custom_call" | custom-call | tf_op jit(solution)/shard_map/pack_chunks/pallas_call | solution.py:298
  59.7 2.7 %convert_element_type.35 = f16[256,16,128]{2,1,0:T(8,128)(2,1)} convert(f32[256,16,128]{2,1,0:T(8,128)} %pack_chunks.1) | non-fusion elementwise | flops 524288 | bytes 3145728 | tf_op jit(solution)/shard_map/convert_element_type | solution.py:487
  62.4 19.3 %all-to-all-start = ((f16[256,16,128]{2,1,0:T(8,128)(2,1)}), f16[256,16,128]{2,1,0:T(8,128)(2,1)S(1)}, u32[]{:S(2)}, u32[]{:S(2)}) async-start(f16[256,16,128]{2,1,0:T(8,128)(2,1)} %convert_element_type.35), calls=%async_computation | async-start | bytes 2097152 | tf_op jit(solution)/shard_map/all_to_all | solution.py:480
  83.0 5.7 %collective-permute-start.6 = (bf16[192,512]{1,0:T(8,128)(2,1)S(1)}, bf16[192,512]{1,0:T(8,128)(2,1)S(1)}, u32[]{:S(2)}, u32[]{:S(2)}) collective-permute-start(bf16[192,512]{1,0:T(8,128)(2,1)S(1)} %copy-done.10), channel_id=1, source_target_pairs={{0,32},{32,64},{64,96},{96,128},{128,160},{160,192},{192,224},{224... | collective-permute-start | bytes 589832 | tf_op jit(solution)/shard_map/ppermute | solution.py:483
  88.7 5.3 %collective-permute-done.5 = bf16[192,512]{1,0:T(8,128)(2,1)S(1)} collective-permute-done((bf16[192,512]{1,0:T(8,128)(2,1)S(1)}, bf16[192,512]{1,0:T(8,128)(2,1)S(1)}, u32[]{:S(2)}, u32[]{:S(2)}) %collective-permute-start.5) | collective-permute-done | bytes 196640 | tf_op jit(solution)/shard_map/ppermute | solution.py:482
  94.0 3.1 %collective-permute-done.6 = bf16[192,512]{1,0:T(8,128)(2,1)S(1)} collective-permute-done((bf16[192,512]{1,0:T(8,128)(2,1)S(1)}, bf16[192,512]{1,0:T(8,128)(2,1)S(1)}, u32[]{:S(2)}, u32[]{:S(2)}) %collective-permute-start.6) | collective-permute-done | bytes 196640 | tf_op jit(solution)/shard_map/ppermute | solution.py:483
  97.1 14.7 %all-to-all-done = f16[256,16,128]{2,1,0:T(8,128)(2,1)S(1)} async-done(((f16[256,16,128]{2,1,0:T(8,128)(2,1)}), f16[256,16,128]{2,1,0:T(8,128)(2,1)S(1)}, u32[]{:S(2)}, u32[]{:S(2)}) %all-to-all-start) | async-done | bytes 1048608 | tf_op jit(solution)/shard_map/all_to_all | solution.py:480
  111.8 1.5 convert_element_type.38.chunks_ref
  113.3 2.8 %finish_chunk.1 = bf16[64,16,128]{2,1,0:T(8,128)(2,1)} custom-call(f32[256,16,128]{2,1,0:T(8,128)} %convert_element_type.38.chunks_ref), custom_call_target="tpu_custom_call" | custom-call | tf_op jit(solution)/shard_map/finish_chunk/pallas_call | solution.py:298
  116.2 10.3 %all-to-all-start.1 = ((bf16[64,16,128]{2,1,0:T(8,128)(2,1)}), bf16[64,16,128]{2,1,0:T(8,128)(2,1)S(1)}, u32[]{:S(2)}, u32[]{:S(2)}) async-start(bf16[64,16,128]{2,1,0:T(8,128)(2,1)} %finish_chunk.1), calls=%async_computation.1 | async-start | bytes 524288 | tf_op jit(solution)/shard_map/all_to_all | solution.py:480
  126.7 2.8 %collective-permute-start.8 = (bf16[16,8,512]{2,1,0:T(8,128)(2,1)S(1)}, bf16[16,8,512]{2,1,0:T(8,128)(2,1)S(1)}, u32[]{:S(2)}, u32[]{:S(2)}) collective-permute-start(bf16[16,8,512]{2,1,0:T(8,128)(2,1)S(1)} %get-tuple-element.50), channel_id=1, source_target_pairs={{1,0},{2,1},{3,2},{4,3},{5,4},{6,5},{7,6},{8,7},{9,8},{10,9},{11,1... | collective-permute-start | bytes 393224 | tf_op jit(solution)/shard_map/ppermute | solution.py:498
  129.5 2.9 %collective-permute-start.7 = (bf16[16,8,512]{2,1,0:T(8,128)(2,1)S(1)}, bf16[16,8,512]{2,1,0:T(8,128)(2,1)S(1)}, u32[]{:S(2)}, u32[]{:S(2)}) collective-permute-start(bf16[16,8,512]{2,1,0:T(8,128)(2,1)S(1)} %get-tuple-element.51), channel_id=1, source_target_pairs={{0,1},{1,2},{2,3},{3,4},{4,5},{5,6},{6,7},{7,8},{8,9},{9,10},{10,1... | collective-permute-start | bytes 393224 | tf_op jit(solution)/shard_map/ppermute | solution.py:497
  133.3 2.4 %collective-permute-done.7 = bf16[16,8,512]{2,1,0:T(8,128)(2,1)S(1)} collective-permute-done((bf16[16,8,512]{2,1,0:T(8,128)(2,1)S(1)}, bf16[16,8,512]{2,1,0:T(8,128)(2,1)S(1)}, u32[]{:S(2)}, u32[]{:S(2)}) %collective-permute-start.7) | collective-permute-done | bytes 131104 | tf_op jit(solution)/shard_map/ppermute | solution.py:497
  135.7 3.6 %all-to-all-done.1.chunks_ref = bf16[64,16,128]{2,1,0:T(8,128)(2,1)S(1)} async-done(((bf16[64,16,128]{2,1,0:T(8,128)(2,1)}), bf16[64,16,128]{2,1,0:T(8,128)(2,1)S(1)}, u32[]{:S(2)}, u32[]{:S(2)}) %all-to-all-start.1) | async-done | bytes 262176 | tf_op jit(solution)/shard_map/all_to_all | solution.py:480
  140.0 2.1 %join_chunks.1 = bf16[4,784,128]{2,1,0:T(8,128)(2,1)} custom-call(bf16[64,16,128]{2,1,0:T(8,128)(2,1)} %copy-done.4), custom_call_target="tpu_custom_call" | custom-call | tf_op jit(solution)/shard_map/join_chunks/pallas_call | solution.py:298
  142.1 12.9 %all_to_all.15.mine_ref = bf16[4,784,128]{2,1,0:T(8,128)(2,1)S(1)} all-to-all(bf16[4,784,128]{2,1,0:T(8,128)(2,1)} %join_chunks.1), channel_id=1, replica_groups={{0,2,32,34},{1,3,33,35},{4,6,36,38},{5,7,37,39},{8,10,40,42},{9,11,41,4..., dimensions={0} | all-to-all | bytes 1605632 | tf_op jit(solution)/shard_map/all_to_all | solution.py:480
  155.0 6.0 %collective-permute-start.9 = (bf16[4,784,128]{2,1,0:T(8,128)(2,1)S(1)}, bf16[4,784,128]{2,1,0:T(8,128)(2,1)S(1)}, u32[]{:S(2)}, u32[]{:S(2)}) collective-permute-start(bf16[4,784,128]{2,1,0:T(8,128)(2,1)S(1)} %all_to_all.15.mine_ref), channel_id=1, source_target_pairs={{0,1},{1,0},{2,3},{3,2},{4,5},{5,4},{6,7},{7,6},{8,9},{9,8},{10,11... | collective-permute-start | bytes 2408456 | tf_op jit(solution)/shard_map/ppermute | solution.py:520
  163.9 2.9 %unpack.1 = (bf16[256,768]{1,0:T(8,128)(2,1)}, bf16[256,256]{1,0:T(8,128)(2,1)}, bf16[256,1024]{1,0:T(8,128)(2,1)}, bf16[1024,256]{1,0:T(8,128)(2,1)}, f32[1,256]{1,0:T(1,128)}, /*index=5*/f32[1,256]{1,0:T(1,128)}) custom-call(s32[2]{0:T(128)} %pad_add_fusion.where_ref, bf16[4,784,128]{2,1,0:T(8,128)(2,1)} %copy-done, bf16[4,784,128]{2,1,0:T(8,128)(2,1)} %copy-done.5), custom_call_target="tpu_custom_call" | custom-call | tf_op jit(solution)/shard_map/unpack/pallas_call | solution.py:298
  (45 shorter events, 12.5 us)
Async XLA Ops:
  1.5 11.6 %collective-permute-start.1 = (bf16[16,8,256]{2,1,0:T(8,128)(2,1)S(1)}, bf16[16,8,256]{2,1,0:T(8,128)(2,1)S(1)}, u32[]{:S(2)}, u32[]{:S(2)}) collective-permute-start(bf16[16,8,256]{2,1,0:T(8,128)(2,1)S(1)} %get-tuple-element.54), channel_id=1, source_target_pairs={{0,1},{1,2},{2,3},{3,4},{4,5},{5,6},{6,7},{7,8},{8,9},{9,10},{10,1... | collective-permute-start | bytes 196616 | tf_op jit(solution)/shard_map/ppermute | solution.py:447
  6.0 7.1 %collective-permute-start = (bf16[16,8,256]{2,1,0:T(8,128)(2,1)S(1)}, bf16[16,8,256]{2,1,0:T(8,128)(2,1)S(1)}, u32[]{:S(2)}, u32[]{:S(2)}) collective-permute-start(bf16[16,8,256]{2,1,0:T(8,128)(2,1)S(1)} %get-tuple-element.55), channel_id=1, source_target_pairs={{1,0},{2,1},{3,2},{4,3},{5,4},{6,5},{7,6},{8,7},{9,8},{10,9},{11,1... | collective-permute-start | bytes 196616 | tf_op jit(solution)/shard_map/ppermute | solution.py:446
  13.2 8.5 %copy-start.2 = (bf16[16,32,256]{2,1,0:T(8,128)(2,1)}, bf16[16,32,256]{2,1,0:T(8,128)(2,1)S(1)}, u32[]{:S(2)}) copy-start(bf16[16,32,256]{2,1,0:T(8,128)(2,1)S(1)} %constant_dynamic-update-slice_fusion) | copy-start | bytes 786436
  13.2 7.5 %collective-permute-start.3 = (bf16[6,32,256]{2,1,0:T(8,128)(2,1)S(1)}, bf16[6,32,256]{2,1,0:T(8,128)(2,1)S(1)}, u32[]{:S(2)}, u32[]{:S(2)}) collective-permute-start(bf16[6,32,256]{2,1,0:T(8,128)(2,1)S(1)} %get-tuple-element.52), channel_id=1, source_target_pairs={{32,0},{64,32},{96,64},{128,96},{160,128},{192,160},{224,192},{256... | collective-permute-start | bytes 294920 | tf_op jit(solution)/shard_map/ppermute | solution.py:449
  14.5 7.1 %collective-permute-start.2 = (bf16[6,32,256]{2,1,0:T(8,128)(2,1)S(1)}, bf16[6,32,256]{2,1,0:T(8,128)(2,1)S(1)}, u32[]{:S(2)}, u32[]{:S(2)}) collective-permute-start(bf16[6,32,256]{2,1,0:T(8,128)(2,1)S(1)} %get-tuple-element.53), channel_id=1, source_target_pairs={{0,32},{32,64},{64,96},{96,128},{128,160},{160,192},{192,224},{224... | collective-permute-start | bytes 294920 | tf_op jit(solution)/shard_map/ppermute | solution.py:450
  20.7 1.0 copy-start.8
  43.3 11.2 %collective-permute-start.4 = (f32[3328,128]{1,0:T(8,128)}, f32[3328,128]{1,0:T(8,128)S(1)}, u32[]{:S(2)}, u32[]{:S(2)}) collective-permute-start(f32[3328,128]{1,0:T(8,128)} %get-tuple-element.33), channel_id=1, source_target_pairs={{0,1},{1,0},{2,3},{3,2},{4,5},{5,4},{6,7},{7,6},{8,9},{9,8},{10,11... | collective-permute-start | bytes 5111816 | tf_op jit(solution)/shard_map/ppermute | solution.py:485
  54.6 1.2 copy-start.1
  62.4 19.3 %copy-start.11 = (bf16[192,512]{1,0:T(8,128)(2,1)S(1)}, bf16[192,512]{1,0:T(8,128)(2,1)}, u32[]{:S(2)}) copy-start(bf16[192,512]{1,0:T(8,128)(2,1)} %get-tuple-element.34) | copy-start | bytes 589828
  62.4 20.6 %copy-start.10 = (bf16[192,512]{1,0:T(8,128)(2,1)S(1)}, bf16[192,512]{1,0:T(8,128)(2,1)}, u32[]{:S(2)}) copy-start(bf16[192,512]{1,0:T(8,128)(2,1)} %get-tuple-element.35) | copy-start | bytes 589828
  62.4 49.3 %all-to-all-start = ((f16[256,16,128]{2,1,0:T(8,128)(2,1)}), f16[256,16,128]{2,1,0:T(8,128)(2,1)S(1)}, u32[]{:S(2)}, u32[]{:S(2)}) async-start(f16[256,16,128]{2,1,0:T(8,128)(2,1)} %convert_element_type.35), calls=%async_computation | async-start | bytes 2097152 | tf_op jit(solution)/shard_map/all_to_all | solution.py:480
  81.7 12.3 %collective-permute-start.5 = (bf16[192,512]{1,0:T(8,128)(2,1)S(1)}, bf16[192,512]{1,0:T(8,128)(2,1)S(1)}, u32[]{:S(2)}, u32[]{:S(2)}) collective-permute-start(bf16[192,512]{1,0:T(8,128)(2,1)S(1)} %copy-done.11), channel_id=1, source_target_pairs={{32,0},{64,32},{96,64},{128,96},{160,128},{192,160},{224,192},{256... | collective-permute-start | bytes 589832 | tf_op jit(solution)/shard_map/ppermute | solution.py:482
  83.0 14.1 %collective-permute-start.6 = (bf16[192,512]{1,0:T(8,128)(2,1)S(1)}, bf16[192,512]{1,0:T(8,128)(2,1)S(1)}, u32[]{:S(2)}, u32[]{:S(2)}) collective-permute-start(bf16[192,512]{1,0:T(8,128)(2,1)S(1)} %copy-done.10), channel_id=1, source_target_pairs={{0,32},{32,64},{64,96},{96,128},{128,160},{160,192},{192,224},{224... | collective-permute-start | bytes 589832 | tf_op jit(solution)/shard_map/ppermute | solution.py:483
  113.3 13.1 %copy-start.3 = (f32[512,512]{1,0:T(8,128)S(1)}, f32[512,512]{1,0:T(8,128)}, u32[]{:S(2)}) copy-start(f32[512,512]{1,0:T(8,128)} %get-tuple-element.31) | copy-start | bytes 3145732
  116.2 23.2 %all-to-all-start.1 = ((bf16[64,16,128]{2,1,0:T(8,128)(2,1)}), bf16[64,16,128]{2,1,0:T(8,128)(2,1)S(1)}, u32[]{:S(2)}, u32[]{:S(2)}) async-start(bf16[64,16,128]{2,1,0:T(8,128)(2,1)} %finish_chunk.1), calls=%async_computation.1 | async-start | bytes 524288 | tf_op jit(solution)/shard_map/all_to_all | solution.py:480
  126.7 6.6 %collective-permute-start.8 = (bf16[16,8,512]{2,1,0:T(8,128)(2,1)S(1)}, bf16[16,8,512]{2,1,0:T(8,128)(2,1)S(1)}, u32[]{:S(2)}, u32[]{:S(2)}) collective-permute-start(bf16[16,8,512]{2,1,0:T(8,128)(2,1)S(1)} %get-tuple-element.50), channel_id=1, source_target_pairs={{1,0},{2,1},{3,2},{4,3},{5,4},{6,5},{7,6},{8,7},{9,8},{10,9},{11,1... | collective-permute-start | bytes 393224 | tf_op jit(solution)/shard_map/ppermute | solution.py:498
  129.5 31.6 %copy-start.6 = (bf16[256,768]{1,0:T(8,128)(2,1)S(1)}, bf16[256,768]{1,0:T(8,128)(2,1)}, u32[]{:S(2)}) copy-start(bf16[256,768]{1,0:T(8,128)(2,1)} %wqkv_ref.1) | copy-start | bytes 1179652
  129.5 31.6 %copy-start.12 = (bf16[256,256]{1,0:T(8,128)(2,1)S(1)}, bf16[256,256]{1,0:T(8,128)(2,1)}, u32[]{:S(2)}) copy-start(bf16[256,256]{1,0:T(8,128)(2,1)} %get-tuple-element.30) | copy-start | bytes 393220
  129.5 6.2 %collective-permute-start.7 = (bf16[16,8,512]{2,1,0:T(8,128)(2,1)S(1)}, bf16[16,8,512]{2,1,0:T(8,128)(2,1)S(1)}, u32[]{:S(2)}, u32[]{:S(2)}) collective-permute-start(bf16[16,8,512]{2,1,0:T(8,128)(2,1)S(1)} %get-tuple-element.51), channel_id=1, source_target_pairs={{0,1},{1,2},{2,3},{3,4},{4,5},{5,6},{6,7},{7,8},{8,9},{9,10},{10,1... | collective-permute-start | bytes 393224 | tf_op jit(solution)/shard_map/ppermute | solution.py:497
  139.3 0.7 copy-start.4
  142.1 19.3 %copy-start.7 = (f32[256,256]{1,0:T(8,128)S(1)}, f32[256,256]{1,0:T(8,128)}, u32[]{:S(2)}) copy-start(f32[256,256]{1,0:T(8,128)} %get-tuple-element.29) | copy-start | bytes 786436
  155.0 8.0 %copy-start = (bf16[4,784,128]{2,1,0:T(8,128)(2,1)}, bf16[4,784,128]{2,1,0:T(8,128)(2,1)S(1)}, u32[]{:S(2)}) copy-start(bf16[4,784,128]{2,1,0:T(8,128)(2,1)S(1)} %all_to_all.15.mine_ref) | copy-start | bytes 2408452
  155.0 7.9 %collective-permute-start.9 = (bf16[4,784,128]{2,1,0:T(8,128)(2,1)S(1)}, bf16[4,784,128]{2,1,0:T(8,128)(2,1)S(1)}, u32[]{:S(2)}, u32[]{:S(2)}) collective-permute-start(bf16[4,784,128]{2,1,0:T(8,128)(2,1)S(1)} %all_to_all.15.mine_ref), channel_id=1, source_target_pairs={{0,1},{1,0},{2,3},{3,2},{4,5},{5,4},{6,7},{7,6},{8,9},{9,8},{10,11... | collective-permute-start | bytes 2408456 | tf_op jit(solution)/shard_map/ppermute | solution.py:520
  162.9 0.9 copy-start.5
  (1 other events, 0.6 us)

commit v4 on v2

--- a/solution.py
+++ b/solution.py
@@ -6,6 +6,7 @@
 from jax.experimental import pallas as pl
 from jax.experimental.pallas import tpu as pltpu
 from jax.sharding import PartitionSpec as P
+
 
 HEADS = 8
 RADIUS = 6
@@ -100,13 +101,16 @@
     side = (core, 1 - core)
 
     def put(index, value):
-        half, row = divmod(index, 6)
-        grads_ref[side[half], row * 512 : row * 512 + 256, :] = value[:, :128]
-        grads_ref[side[half], row * 512 + 256 : row * 512 + 512, :] = value[:, 128:]
+        half, block = divmod(index, 6)
+        for right in range(2):
+            k, at = divmod(2 * block + right, 3)
+            grads_ref[side[half], k, at * 256 : (at + 1) * 256, :] = value[:, right * 128 : (right + 1) * 128]
 
     def put_gain(half, terms):
-        column = jnp.sum(terms.T, axis=1, keepdims=True)
-        grads_ref[side[half], 3072:, :] = jnp.broadcast_to(column, (width, 128))
+        column = jnp.broadcast_to(jnp.sum(terms.T, axis=1, keepdims=True), (width, 128))
+        each = width // 4
+        for k in range(4):
+            grads_ref[side[half], k, 768:, :] = column[k * each : (k + 1) * each]
 
     rim = RADIUS * across
     inner = rows * across
@@ -260,8 +264,8 @@
         shape((rim, 2 * width), BF16),
         shape((rim, 2 * width), BF16),
         shape((rows * across, 2 * width), F32),
-        shape((3072 + width, 128), F32),
-        shape((3072 + width, 128), F32),
+        shape((4, 768 + width // 4, 128), F32),
+        shape((4, 768 + width // 4, 128), F32),
     ]
     return pl.pallas_call(
         functools.partial(local_kernel, dims),
@@ -269,7 +273,7 @@
         in_specs=[pl.BlockSpec(memory_space=pltpu.SMEM)] + [vmem] * 11,
         out_specs=[vmem] * len(outs),
         scratch_shapes=[
-            pltpu.VMEM((2, 3072 + width, 128), F32),
+            pltpu.VMEM((2, 4, 768 + width // 4, 128), F32),
             pltpu.VMEM((grid, width), BF16),
             pltpu.VMEM((grid, width), BF16),
             pltpu.VMEM((grid, width), BF16),
@@ -291,7 +295,7 @@
     )(where, frame, wide, top, bottom, *weights, cotangent)
 
 
-def small_kernel(body, name, outs, *args):
+def small_kernel(body, outs, *args, scratch=()):
     vmem = pl.BlockSpec(memory_space=pltpu.VMEM)
     smem = pl.BlockSpec(memory_space=pltpu.SMEM)
     return pl.pallas_call(
@@ -299,7 +303,7 @@
         out_shape=outs,
         in_specs=[smem if a.dtype == jnp.int32 else vmem for a in args],
         out_specs=jax.tree.map(lambda _: vmem, outs),
-        name=name,
+        scratch_shapes=scratch,
     )(*args)
 
 
@@ -307,29 +311,21 @@
     return lax.broadcasted_iota(jnp.int32, shape, 1)
 
 
-def pack_chunks(n, parts_ref, chunks_ref):
-    total = parts_ref[0]
-    for k in range(1, parts_ref.shape[0]):
-        total = total + parts_ref[k]
-    deep = 512 // n
-    chunks_ref[:, :deep] = total[:512].reshape(n, deep, 128)
-    half = n // 2
-    tail = total[512:768].reshape(half, deep, 128)
-    gain = total[768:].reshape(n, -1, 128)[:, :1]
-    row = first_rows(tail.shape)
-    for i in range(2):
-        piece = tail if i == 0 else pltpu.roll(tail, deep // 2, 1)
-        mine = gain[i * half : (i + 1) * half]
-        chunks_ref[i * half : (i + 1) * half, deep:] = jnp.where(row < deep // 2, piece, mine)
-
-
-def finish_chunk(scale, chunks_ref, own_ref):
-    n, deep = chunks_ref.shape[0], chunks_ref.shape[1] // 2
-    total = jnp.sum(chunks_ref[...], axis=0) * scale
-    high = total.astype(BF16).astype(F32)
+def deal_chunks(parts, n):
+    total = jnp.sum(parts, axis=0)
+    body = total[:512].reshape(n, 8, 128)
+    tail = total[512:768].reshape(n // 2, 8, 128)
+    tail = jnp.concatenate([tail[:, :4], tail[:, 4:]], axis=0)
+    gain = jnp.broadcast_to(total[768:].reshape(n, 1, 128), (n, 4, 128))
+    return jnp.concatenate([body, tail, gain], axis=1)
+
+
+def finish_chunk(chunks, scale):
+    total = jnp.sum(chunks, axis=0) * scale
+    high = total.astype(BF16)
+    low = (total - high.astype(F32)).astype(BF16)
     row = lax.broadcasted_iota(jnp.int32, total.shape, 0)
-    total = jnp.where(row == total.shape[0] - 1, total - high, total).astype(BF16)
-    own_ref[...] = jnp.broadcast_to(total[None], (n,) + total.shape)
+    return jnp.broadcast_to(jnp.where(row == 15, low, high)[None], chunks.shape)
 
 
 def join_chunks(chunks_ref, rows_ref):
@@ -368,9 +364,11 @@
                 target, column = qkv_ref, 0
             lane = column * 256 + right * 128
             target[:, lane : lane + 128] = value
-        for k in range(rows_ref.shape[0]):
-            gain = rows_ref[k, 768:, :].astype(F32)
-            gain_ref[k : k + 1, :] = (gain + pltpu.roll(gain, 64, 1))[:1]
+        lane = lax.broadcasted_iota(jnp.int32, (16, 128), 1)
+        for k in range(0, rows_ref.shape[0], 2):
+            gain = [rows_ref[k + i, 768:, :].astype(F32) for i in range(2)]
+            gain = [g + pltpu.roll(g, 64, 1) for g in gain]
+            gain_ref[:, k * 64 : k * 64 + 128] = jnp.where(lane < 64, *gain)[:1]
 
     @pl.when(where_ref[1] == 0)
     def _():
@@ -455,10 +453,7 @@
     down = lax.ppermute(down, "lat", south)
 
     other = lax.ppermute(send, both, swap)
-    pieces = (keep[:3072] + other[:3072]).reshape(n_x, 768, 128)
-    tails = (keep[3072:] + other[3072:]).reshape(n_x, -1, 128)
-    parts = exchange(jnp.concatenate([pieces, tails], axis=1), over_x)
-    parts, up, down = lax.optimization_barrier((parts, up, down))
+    parts = exchange(keep + other, over_x)
 
     up = up.reshape(RADIUS, across, 2 * width).astype(F32)
     down = down.reshape(RADIUS, across, 2 * width).astype(F32)
@@ -469,13 +464,10 @@
     to_west = centre[:, cols + EDGE :].astype(BF16)
     from_west = lax.ppermute(to_east, "lon", east)
     from_east = lax.ppermute(to_west, "lon", west)
-
-    deep = 2 * 512 // n_yz
-    chunks = small_kernel(
-        functools.partial(pack_chunks, n_yz), "pack_chunks", shape((n_yz, deep, 128), F32), parts
-    )
-    chunks = exchange(chunks, over_yz)
+    chunks = exchange(deal_chunks(parts, n_yz), over_yz)
     chunks, from_west, from_east = lax.optimization_barrier((chunks, from_west, from_east))
+
+    own = exchange(finish_chunk(chunks, grad_scale), over_yz)
 
     rest = cols - EDGE
     owned = (
@@ -486,29 +478,24 @@
     d_projected = jnp.concatenate([dq, owned.reshape(tokens, 2 * width).astype(BF16)], axis=1)
     grad_frame = (d_mid + nt(d_projected, weight_qkv)).astype(BF16)
 
-    own = small_kernel(
-        functools.partial(finish_chunk, grad_scale), "finish_chunk", shape((n_yz, deep, 128), BF16), chunks
-    )
-    own = exchange(own, over_yz)
-    mine = small_kernel(join_chunks, "join_chunks", shape((n_x, 784, 128), BF16), own)
+    mine = small_kernel(join_chunks, shape((n_x, 784, 128), BF16), own)
     mine = exchange(mine, over_x)
     theirs = lax.ppermute(mine, both, swap)
     gradients = small_kernel(
         unpack,
-        "unpack",
         [
             shape((width, 3 * width), BF16),
             shape((width, width), BF16),
             shape((width, ff), BF16),
             shape((ff, width), BF16),
-            shape((n_x, 128), F32),
-            shape((n_x, 128), F32),
+            shape((1, width), F32),
+            shape((1, width), F32),
         ],
         where,
         mine,
         theirs,
     )
-    gain_sums = [g[:, : width // n_x].reshape(width) for g in gradients[4:]]
+    gain_sums = [g.reshape(width) for g in gradients[4:]]
     return (
         block_out.reshape(rows, cols, width),
         grad_frame.reshape(rows, cols, width),

time: 184 us -> 177 us (0.962)
  blocking collectives: 36.8 us -> 67.8 us
  waiting for transfers between devices: 35.7 us -> 12.1 us
  local copies, waits for them, and re-layouts: 8.09 us -> 3.59 us
  starting transfers between devices: 65.1 us -> 60.8 us
  Pallas kernels: 30.2 us -> 26 us
    all_to_all x2 -> x3, blocking collectives: 36.8 us -> 67.8 us  [exchange(): return lax.all_to_all(blocks, both, 0, 0, axis_index_groups=groups)]
    ppermute x1, waiting for transfers between devices: 18.8 us -> 1.53 us  [on_device(): up = lax.ppermute(up, 'lat', north)]
    all_to_all x2 -> x1, starting transfers between devices: 22.9 us -> 13.9 us  [exchange(): return lax.all_to_all(blocks, both, 0, 0, axis_index_groups=groups)]
    all_to_all x2 -> x1, waiting for transfers between devices: 8.89 us -> 0.01 us  [exchange(): return lax.all_to_all(blocks, both, 0, 0, axis_index_groups=groups)]
    pallas_call x4 -> x2, Pallas kernels: 9.16 us -> 4.95 us  [small_kernel(): pl.pallas_call(body, out_shape=outs, in_specs=[smem if a.dtype == jnp.int...]
    ppermute x1, starting transfers between devices: 4.52 us -> 8.5 us  [on_device(): theirs = lax.ppermute(mine, both, swap)]
    reshape x2, local copies, waits for them, and re-layouts: 2.62 us -> 0.03 us  [the longest x1 0.02 us: deal_chunks(): body = total[:512].reshape(n, 8, 128)]
    ppermute x1, waiting for transfers between devices: 1 us -> 3.23 us  [on_device(): from_east = lax.ppermute(to_west, 'lon', west)]
  transfers between devices with their start and end apart: 12 -> 11, of which waited for: 8 -> 7; matrix products, arithmetic and copies ran while one was open for 2% -> 2% of each run, Pallas kernels for 0% -> 0%
where the time goes in v4:
time: 177 us; the launch traced here: 176 us
  blocking collectives  67.8 us (38%)
  starting transfers between devices  60.8 us (34%)
  Pallas kernels  26 us (15%)
  waiting for transfers between devices  12.1 us (7%)
  other arithmetic  4.46 us (3%)
  local copies, waits for them, and re-layouts  3.59 us (2%)
    all_to_all x3, blocking collectives, exchange(): return lax.all_to_all(blocks, both, 0, 0, axis_index_groups=groups)  67.8 us
    pallas_call x1, Pallas kernels, local_part(): pl.pallas_call(functools.partial(local_kernel, dims), out_shape=outs, in_...  21 us
    all_to_all x1, starting transfers between devices, exchange(): return lax.all_to_all(blocks, both, 0, 0, axis_index_groups=groups)  13.9 us
    ppermute x1, starting transfers between devices, on_device(): theirs = lax.ppermute(mine, both, swap)  8.5 us
    ppermute x1, starting transfers between devices, on_device(): other = lax.ppermute(send, both, swap)  7.8 us
    ppermute x1, starting transfers between devices, on_device(): from_east = lax.ppermute(frame[:, :EDGE], 'lon', west)  6.17 us
    ppermute x1, starting transfers between devices, on_device(): down = lax.ppermute(down, 'lat', south)  5.5 us
    ppermute x1, starting transfers between devices, on_device(): top = lax.ppermute(wide[rows - RADIUS:], 'lat', south)  5.5 us
  transfers between devices with their start and end apart: 11, of which 7 were waited for; matrix products, arithmetic and copies ran while one was open for 2% of the time, Pallas kernels for 0%

profile of v4, /device:TPU:1, one launch (start us, length us, event | category | flops | bytes accessed | tf_op | source)
XLA Modules:
  0.0 176.0 jit_solution(10046539350131198231)
XLA Ops:
  1.5 4.5 %collective-permute-start.1 = (bf16[16,8,256]{2,1,0:T(8,128)(2,1)S(1)}, bf16[16,8,256]{2,1,0:T(8,128)(2,1)S(1)}, u32[]{:S(2)}, u32[]{:S(2)}) collective-permute-start(bf16[16,8,256]{2,1,0:T(8,128)(2,1)S(1)} %get-tuple-element.50), channel_id=1, source_target_pairs={{0,1},{1,2},{2,3},{3,4},{4,5},{5,6},{6,7},{7,8},{8,9},{9,10},{10,1... | collective-permute-start | bytes 196616 | tf_op jit(solution)/shard_map/ppermute | solution.py:417
  6.0 6.2 %collective-permute-start = (bf16[16,8,256]{2,1,0:T(8,128)(2,1)S(1)}, bf16[16,8,256]{2,1,0:T(8,128)(2,1)S(1)}, u32[]{:S(2)}, u32[]{:S(2)}) collective-permute-start(bf16[16,8,256]{2,1,0:T(8,128)(2,1)S(1)} %get-tuple-element.51), channel_id=1, source_target_pairs={{1,0},{2,1},{3,2},{4,3},{5,4},{6,5},{7,6},{8,7},{9,8},{10,9},{11,1... | collective-permute-start | bytes 196616 | tf_op jit(solution)/shard_map/ppermute | solution.py:416
  13.2 1.3 collective-permute-start.3
  14.5 5.5 %collective-permute-start.2 = (bf16[6,32,256]{2,1,0:T(8,128)(2,1)S(1)}, bf16[6,32,256]{2,1,0:T(8,128)(2,1)S(1)}, u32[]{:S(2)}, u32[]{:S(2)}) collective-permute-start(bf16[6,32,256]{2,1,0:T(8,128)(2,1)S(1)} %get-tuple-element.47), channel_id=1, source_target_pairs={{0,32},{32,64},{64,96},{96,128},{128,160},{160,192},{192,224},{224... | collective-permute-start | bytes 294920 | tf_op jit(solution)/shard_map/ppermute | solution.py:420
  20.7 1.0 collective-permute-done.2
  22.3 21.0 %local_part.1 = (bf16[256,256]{1,0:T(8,128)(2,1)}, f32[256,256]{1,0:T(8,128)}, bf16[256,256]{1,0:T(8,128)(2,1)}, bf16[192,512]{1,0:T(8,128)(2,1)}, bf16[192,512]...) custom-call(s32[2]{0:T(128)} %pad_add_fusion.where_ref, ...), custom_call_target="tpu_custom_call" | custom-call | tf_op jit(solution)/shard_map/local_part/pallas_call | solution.py:270
  43.3 7.8 %collective-permute-start.6 = (f32[4,832,128]{2,1,0:T(8,128)}, f32[4,832,128]{2,1,0:T(8,128)S(1)}, u32[]{:S(2)}, u32[]{:S(2)}) collective-permute-start(f32[4,832,128]{2,1,0:T(8,128)} %get-tuple-element.32), channel_id=1, source_target_pairs={{0,1},{1,0},{2,3},{3,2},{4,5},{5,4},{6,7},{7,6},{8,9},{9,8},{10,11... | collective-permute-start | bytes 5111816 | tf_op jit(solution)/shard_map/ppermute | solution.py:455
  51.1 3.4 %collective-permute-done.6 = f32[4,832,128]{2,1,0:T(8,128)S(1)} collective-permute-done((f32[4,832,128]{2,1,0:T(8,128)}, f32[4,832,128]{2,1,0:T(8,128)S(1)}, u32[]{:S(2)}, u32[]{:S(2)}) %collective-permute-start.6) | collective-permute-done | bytes 1703968 | tf_op jit(solution)/shard_map/ppermute | solution.py:455
  54.5 1.7 add.33
  56.2 26.0 %all_to_all.20 = f32[4,832,128]{2,1,0:T(8,128)S(1)} all-to-all(f32[4,832,128]{2,1,0:T(8,128)S(1)} %add.33), channel_id=1, replica_groups={{0,2,32,34},{1,3,33,35},{4,6,36,38},{5,7,37,39},{8,10,40,42},{9,11,41,4..., dimensions={0} | all-to-all | bytes 3407872 | tf_op jit(solution)/shard_map/all_to_all | solution.py:450
  83.3 13.9 %all-to-all-start.1 = ((f32[64,16,128]{2,1,0:T(8,128)}), f32[64,16,128]{2,1,0:T(8,128)S(1)}, u32[]{:S(2)}, u32[]{:S(2)}) async-start(f32[64,16,128]{2,1,0:T(8,128)} %pad_maximum_fusion), calls=%async_computation.1 | async-start | bytes 1048576 | tf_op jit(solution)/shard_map/all_to_all | solution.py:450
  97.2 1.3 collective-permute-start.4
  98.5 5.5 %collective-permute-start.5 = (bf16[192,512]{1,0:T(8,128)(2,1)S(1)}, bf16[192,512]{1,0:T(8,128)(2,1)S(1)}, u32[]{:S(2)}, u32[]{:S(2)}) collective-permute-start(bf16[192,512]{1,0:T(8,128)(2,1)S(1)} %copy-done.8), channel_id=1, source_target_pairs={{0,32},{32,64},{64,96},{96,128},{128,160},{160,192},{192,224},{224... | collective-permute-start | bytes 589832 | tf_op jit(solution)/shard_map/ppermute | solution.py:453
  104.0 1.5 collective-permute-done.4
  105.6 1.8 %collective-permute-done.5 = bf16[192,512]{1,0:T(8,128)(2,1)S(1)} collective-permute-done((bf16[192,512]{1,0:T(8,128)(2,1)S(1)}, bf16[192,512]{1,0:T(8,128)(2,1)S(1)}, u32[]{:S(2)}, u32[]{:S(2)}) %collective-permute-start.5) | collective-permute-done | bytes 196640 | tf_op jit(solution)/shard_map/ppermute | solution.py:453
  107.6 4.3 %collective-permute-start.8 = (bf16[16,8,512]{2,1,0:T(8,128)(2,1)S(1)}, bf16[16,8,512]{2,1,0:T(8,128)(2,1)S(1)}, u32[]{:S(2)}, u32[]{:S(2)}) collective-permute-start(bf16[16,8,512]{2,1,0:T(8,128)(2,1)S(1)} %get-tuple-element.44), channel_id=1, source_target_pairs={{1,0},{2,1},{3,2},{4,3},{5,4},{6,5},{7,6},{8,7},{9,8},{10,9},{11,1... | collective-permute-start | bytes 393224 | tf_op jit(solution)/shard_map/ppermute | solution.py:466
  111.9 2.1 %collective-permute-start.7 = (bf16[16,8,512]{2,1,0:T(8,128)(2,1)S(1)}, bf16[16,8,512]{2,1,0:T(8,128)(2,1)S(1)}, u32[]{:S(2)}, u32[]{:S(2)}) collective-permute-start(bf16[16,8,512]{2,1,0:T(8,128)(2,1)S(1)} %get-tuple-element.45), channel_id=1, source_target_pairs={{0,1},{1,2},{2,3},{3,4},{4,5},{5,6},{6,7},{7,8},{8,9},{9,10},{10,1... | collective-permute-start | bytes 393224 | tf_op jit(solution)/shard_map/ppermute | solution.py:465
  114.0 3.2 %collective-permute-done.8 = bf16[16,8,512]{2,1,0:T(8,128)(2,1)S(1)} collective-permute-done((bf16[16,8,512]{2,1,0:T(8,128)(2,1)S(1)}, bf16[16,8,512]{2,1,0:T(8,128)(2,1)S(1)}, u32[]{:S(2)}, u32[]{:S(2)}) %collective-permute-start.8) | collective-permute-done | bytes 131104 | tf_op jit(solution)/shard_map/ppermute | solution.py:466
  117.8 28.9 %all_to_all.21.chunks_ref = bf16[64,16,128]{2,1,0:T(8,128)(2,1)} all-to-all(bf16[64,16,128]{2,1,0:T(8,128)(2,1)S(1)} %broadcast_in_dim.5), channel_id=1, replica_groups={{0,4,8,12,16,20,24,28,64,68,72,76,80,84,88,92,128,132,136,140,144,148,1..., dimensions={0} | all-to-all | bytes 524288 | tf_op jit(solution)/shard_map/all_to_all | solution.py:450
  146.7 2.1 %shard_map.143 = bf16[4,784,128]{2,1,0:T(8,128)(2,1)} custom-call(bf16[64,16,128]{2,1,0:T(8,128)(2,1)} %all_to_all.21.chunks_ref), custom_call_target="tpu_custom_call" | custom-call | tf_op jit(solution)/shard_map/pallas_call | solution.py:301
  148.8 13.0 %all_to_all.22.mine_ref = bf16[4,784,128]{2,1,0:T(8,128)(2,1)S(1)} all-to-all(bf16[4,784,128]{2,1,0:T(8,128)(2,1)} %shard_map.143), channel_id=1, replica_groups={{0,2,32,34},{1,3,33,35},{4,6,36,38},{5,7,37,39},{8,10,40,42},{9,11,41,4..., dimensions={0} | all-to-all | bytes 1605632 | tf_op jit(solution)/shard_map/all_to_all | solution.py:450
  161.8 8.5 %collective-permute-start.9 = (bf16[4,784,128]{2,1,0:T(8,128)(2,1)S(1)}, bf16[4,784,128]{2,1,0:T(8,128)(2,1)S(1)}, u32[]{:S(2)}, u32[]{:S(2)}) collective-permute-start(bf16[4,784,128]{2,1,0:T(8,128)(2,1)S(1)} %all_to_all.22.mine_ref), channel_id=1, source_target_pairs={{0,1},{1,0},{2,3},{3,2},{4,5},{5,4},{6,7},{7,6},{8,9},{9,8},{10,11... | collective-permute-start | bytes 2408456 | tf_op jit(solution)/shard_map/ppermute | solution.py:483
  172.2 0.9 copy-done.3
  173.2 2.9 %shard_map.144 = (bf16[256,768]{1,0:T(8,128)(2,1)}, bf16[256,256]{1,0:T(8,128)(2,1)}, bf16[256,1024]{1,0:T(8,128)(2,1)}, bf16[1024,256]{1,0:T(8,128)(2,1)}, f32[1,256]{1,0:T(1,128)}, /*index=5*/f32[1,256]{1,0:T(1,128)}) custom-call(s32[2]{0:T(128)} %pad_add_fusion.where_ref, bf16[4,784,128]{2,1,0:T(8,128)(2,1)} %copy-done, bf16[4,784,128]{2,1,0:T(8,128)(2,1)} %copy-done.3), custom_call_target="tpu_custom_call" | custom-call | tf_op jit(solution)/shard_map/pallas_call | solution.py:301
  (49 shorter events, 6.9 us)
Async XLA Ops:
  1.5 11.6 %collective-permute-start.1 = (bf16[16,8,256]{2,1,0:T(8,128)(2,1)S(1)}, bf16[16,8,256]{2,1,0:T(8,128)(2,1)S(1)}, u32[]{:S(2)}, u32[]{:S(2)}) collective-permute-start(bf16[16,8,256]{2,1,0:T(8,128)(2,1)S(1)} %get-tuple-element.50), channel_id=1, source_target_pairs={{0,1},{1,2},{2,3},{3,4},{4,5},{5,6},{6,7},{7,8},{8,9},{9,10},{10,1... | collective-permute-start | bytes 196616 | tf_op jit(solution)/shard_map/ppermute | solution.py:417
  6.0 7.1 %collective-permute-start = (bf16[16,8,256]{2,1,0:T(8,128)(2,1)S(1)}, bf16[16,8,256]{2,1,0:T(8,128)(2,1)S(1)}, u32[]{:S(2)}, u32[]{:S(2)}) collective-permute-start(bf16[16,8,256]{2,1,0:T(8,128)(2,1)S(1)} %get-tuple-element.51), channel_id=1, source_target_pairs={{1,0},{2,1},{3,2},{4,3},{5,4},{6,5},{7,6},{8,7},{9,8},{10,9},{11,1... | collective-permute-start | bytes 196616 | tf_op jit(solution)/shard_map/ppermute | solution.py:416
  13.2 8.5 %copy-start.1 = (bf16[16,32,256]{2,1,0:T(8,128)(2,1)}, bf16[16,32,256]{2,1,0:T(8,128)(2,1)S(1)}, u32[]{:S(2)}) copy-start(bf16[16,32,256]{2,1,0:T(8,128)(2,1)S(1)} %constant_dynamic-update-slice_fusion) | copy-start | bytes 786436
  13.2 7.5 %collective-permute-start.3 = (bf16[6,32,256]{2,1,0:T(8,128)(2,1)S(1)}, bf16[6,32,256]{2,1,0:T(8,128)(2,1)S(1)}, u32[]{:S(2)}, u32[]{:S(2)}) collective-permute-start(bf16[6,32,256]{2,1,0:T(8,128)(2,1)S(1)} %get-tuple-element.46), channel_id=1, source_target_pairs={{32,0},{64,32},{96,64},{128,96},{160,128},{192,160},{224,192},{256... | collective-permute-start | bytes 294920 | tf_op jit(solution)/shard_map/ppermute | solution.py:419
  14.5 7.1 %collective-permute-start.2 = (bf16[6,32,256]{2,1,0:T(8,128)(2,1)S(1)}, bf16[6,32,256]{2,1,0:T(8,128)(2,1)S(1)}, u32[]{:S(2)}, u32[]{:S(2)}) collective-permute-start(bf16[6,32,256]{2,1,0:T(8,128)(2,1)S(1)} %get-tuple-element.47), channel_id=1, source_target_pairs={{0,32},{32,64},{64,96},{96,128},{128,160},{160,192},{192,224},{224... | collective-permute-start | bytes 294920 | tf_op jit(solution)/shard_map/ppermute | solution.py:420
  20.7 1.0 copy-start.6
  21.6 0.6 copy-start.7
  43.3 11.2 %collective-permute-start.6 = (f32[4,832,128]{2,1,0:T(8,128)}, f32[4,832,128]{2,1,0:T(8,128)S(1)}, u32[]{:S(2)}, u32[]{:S(2)}) collective-permute-start(f32[4,832,128]{2,1,0:T(8,128)} %get-tuple-element.32), channel_id=1, source_target_pairs={{0,1},{1,0},{2,3},{3,2},{4,5},{5,4},{6,7},{7,6},{8,9},{9,8},{10,11... | collective-permute-start | bytes 5111816 | tf_op jit(solution)/shard_map/ppermute | solution.py:455
  82.3 14.9 %copy-start.9 = (bf16[192,512]{1,0:T(8,128)(2,1)S(1)}, bf16[192,512]{1,0:T(8,128)(2,1)}, u32[]{:S(2)}) copy-start(bf16[192,512]{1,0:T(8,128)(2,1)} %get-tuple-element.29) | copy-start | bytes 589828
  82.3 16.2 %copy-start.8 = (bf16[192,512]{1,0:T(8,128)(2,1)S(1)}, bf16[192,512]{1,0:T(8,128)(2,1)}, u32[]{:S(2)}) copy-start(bf16[192,512]{1,0:T(8,128)(2,1)} %get-tuple-element.30) | copy-start | bytes 589828
  82.3 25.0 %copy-start.2 = (f32[512,512]{1,0:T(8,128)S(1)}, f32[512,512]{1,0:T(8,128)}, u32[]{:S(2)}) copy-start(f32[512,512]{1,0:T(8,128)} %get-tuple-element.28) | copy-start | bytes 3145732
  83.3 34.3 %all-to-all-start.1 = ((f32[64,16,128]{2,1,0:T(8,128)}), f32[64,16,128]{2,1,0:T(8,128)S(1)}, u32[]{:S(2)}, u32[]{:S(2)}) async-start(f32[64,16,128]{2,1,0:T(8,128)} %pad_maximum_fusion), calls=%async_computation.1 | async-start | bytes 1048576 | tf_op jit(solution)/shard_map/all_to_all | solution.py:450
  97.2 8.4 %collective-permute-start.4 = (bf16[192,512]{1,0:T(8,128)(2,1)S(1)}, bf16[192,512]{1,0:T(8,128)(2,1)S(1)}, u32[]{:S(2)}, u32[]{:S(2)}) collective-permute-start(bf16[192,512]{1,0:T(8,128)(2,1)S(1)} %copy-done.9), channel_id=1, source_target_pairs={{32,0},{64,32},{96,64},{128,96},{160,128},{192,160},{224,192},{256... | collective-permute-start | bytes 589832 | tf_op jit(solution)/shard_map/ppermute | solution.py:452
  98.5 8.8 %collective-permute-start.5 = (bf16[192,512]{1,0:T(8,128)(2,1)S(1)}, bf16[192,512]{1,0:T(8,128)(2,1)S(1)}, u32[]{:S(2)}, u32[]{:S(2)}) collective-permute-start(bf16[192,512]{1,0:T(8,128)(2,1)S(1)} %copy-done.8), channel_id=1, source_target_pairs={{0,32},{32,64},{64,96},{96,128},{128,160},{160,192},{192,224},{224... | collective-permute-start | bytes 589832 | tf_op jit(solution)/shard_map/ppermute | solution.py:453
  107.6 9.7 %collective-permute-start.8 = (bf16[16,8,512]{2,1,0:T(8,128)(2,1)S(1)}, bf16[16,8,512]{2,1,0:T(8,128)(2,1)S(1)}, u32[]{:S(2)}, u32[]{:S(2)}) collective-permute-start(bf16[16,8,512]{2,1,0:T(8,128)(2,1)S(1)} %get-tuple-element.44), channel_id=1, source_target_pairs={{1,0},{2,1},{3,2},{4,3},{5,4},{6,5},{7,6},{8,7},{9,8},{10,9},{11,1... | collective-permute-start | bytes 393224 | tf_op jit(solution)/shard_map/ppermute | solution.py:466
  111.9 5.7 %collective-permute-start.7 = (bf16[16,8,512]{2,1,0:T(8,128)(2,1)S(1)}, bf16[16,8,512]{2,1,0:T(8,128)(2,1)S(1)}, u32[]{:S(2)}, u32[]{:S(2)}) collective-permute-start(bf16[16,8,512]{2,1,0:T(8,128)(2,1)S(1)} %get-tuple-element.45), channel_id=1, source_target_pairs={{0,1},{1,2},{2,3},{3,4},{4,5},{5,6},{6,7},{7,8},{8,9},{9,10},{10,1... | collective-permute-start | bytes 393224 | tf_op jit(solution)/shard_map/ppermute | solution.py:465
  146.7 23.7 %copy-start.4 = (bf16[256,768]{1,0:T(8,128)(2,1)S(1)}, bf16[256,768]{1,0:T(8,128)(2,1)}, u32[]{:S(2)}) copy-start(bf16[256,768]{1,0:T(8,128)(2,1)} %wqkv_ref.1) | copy-start | bytes 1179652
  146.7 23.7 %copy-start.10 = (bf16[256,256]{1,0:T(8,128)(2,1)S(1)}, bf16[256,256]{1,0:T(8,128)(2,1)}, u32[]{:S(2)}) copy-start(bf16[256,256]{1,0:T(8,128)(2,1)} %get-tuple-element.27) | copy-start | bytes 393220
  148.8 21.9 %copy-start.5 = (f32[256,256]{1,0:T(8,128)S(1)}, f32[256,256]{1,0:T(8,128)}, u32[]{:S(2)}) copy-start(f32[256,256]{1,0:T(8,128)} %get-tuple-element.26) | copy-start | bytes 786436
  161.8 10.4 %copy-start = (bf16[4,784,128]{2,1,0:T(8,128)(2,1)}, bf16[4,784,128]{2,1,0:T(8,128)(2,1)S(1)}, u32[]{:S(2)}) copy-start(bf16[4,784,128]{2,1,0:T(8,128)(2,1)S(1)} %all_to_all.22.mine_ref) | copy-start | bytes 2408452
  161.8 10.4 %collective-permute-start.9 = (bf16[4,784,128]{2,1,0:T(8,128)(2,1)S(1)}, bf16[4,784,128]{2,1,0:T(8,128)(2,1)S(1)}, u32[]{:S(2)}, u32[]{:S(2)}) collective-permute-start(bf16[4,784,128]{2,1,0:T(8,128)(2,1)S(1)} %all_to_all.22.mine_ref), channel_id=1, source_target_pairs={{0,1},{1,0},{2,3},{3,2},{4,5},{5,4},{6,7},{7,6},{8,9},{9,8},{10,11... | collective-permute-start | bytes 2408456 | tf_op jit(solution)/shard_map/ppermute | solution.py:483
  172.2 0.9 copy-start.3
